TPU v7x, 512 devices: a whole 4x8x8 slice. The times are simulated.
512 devices in a mesh: fsdp: 32 (over z_lo, x, core), cp: 16 (over y, z_hi).
Axes of the slice: x: 4, y: 8, z: 8 (z_hi: 2, z_lo: 4; z = z_hi * 4 + z_lo), core: 2. Of those that a mesh axis runs over, the one named last changes fastest.
Arguments:
- queries: bfloat16 [4096, 16384], P('cp', 'fsdp'), may hold values from -8 to 8
- key_vectors: bfloat16 [4096, 1024], P(('fsdp', 'cp')), may hold values from -8 to 8
- value_vectors: bfloat16 [4096, 1024], P(('fsdp', 'cp')), may hold values from -6 to 6
- out_grads: bfloat16 [4096, 16384], P('cp', 'fsdp'), may hold values from -6 to 6
- pair_order: int32 [32], replicated, may hold values from 0 to 31, as said below
Outputs:
- attended: bfloat16 [4096, 16384], P('cp', 'fsdp')
- query_grads: bfloat16 [4096, 16384], P('cp', 'fsdp')
- key_grads: float32 [4096, 1024], P(('fsdp', 'cp'))
- value_grads: float32 [4096, 1024], P(('fsdp', 'cp'))
Inputs may be any that keep to these rules, and one draw needn't show every extreme that they name: `pair_order`: A permutation of the stretches; slots 2 c and 2 c + 1 hold stretches P and 31 - P for some P, in either order.
All inputs are finite; a program needn't handle non-finite values.
Results may differ from a plain program's by a relative error of at most 0.034.
Values may be sent and summed in bfloat16 or wider, within the bound.
No kernel may reach another device: no remote copies, remote signals or barrier semaphores. Data moves between devices by JAX's collectives and lax.ppermute only.
A program may use at most 64 MiB of HBM per device.

v0:
```python
import math

import jax
import jax.numpy as jnp
from jax import lax
from jax.sharding import PartitionSpec as P

HD = 128


NEG_FILL = -1e30


def block_scores(query_rows, key_part, positions, key_start, score_scale):
    scores = (
        jnp.einsum("nhd,jd->hnj", query_rows, key_part, preferred_element_type=jnp.float32)
        * score_scale
    )
    key_positions = key_start + jnp.arange(key_part.shape[0], dtype=jnp.int32)
    visible = key_positions[None, :] <= positions[:, None]
    return (scores, visible[None, :, :])


def attend(whole_k, whole_v, query_rows, positions, blocks, block_width):
    row_count, head_count, head_dim = query_rows.shape
    score_scale = 1.0 / math.sqrt(head_dim)

    def online_step(block_index, state_three):
        row_peak, row_total, value_sum = state_three
        key_start = block_index * block_width
        key_part = lax.dynamic_slice_in_dim(whole_k, key_start, block_width, 0)
        value_part = lax.dynamic_slice_in_dim(whole_v, key_start, block_width, 0)
        scores, visible = block_scores(query_rows, key_part, positions, key_start, score_scale)
        masked = jnp.where(visible, scores, NEG_FILL)
        new_peak = jnp.maximum(row_peak, jnp.max(masked, axis=2))
        factor = jnp.exp(row_peak - new_peak)
        weights = jnp.where(visible, jnp.exp(masked - new_peak[:, :, None]), 0.0)
        row_total = row_total * factor + jnp.sum(weights, axis=2)
        weight_half = weights.astype(jnp.bfloat16)
        block_sum = jnp.einsum(
            "hnj,jd->nhd", weight_half, value_part, preferred_element_type=jnp.float32
        )
        value_sum = value_sum * factor.T[:, :, None] + block_sum
        return (new_peak, row_total, value_sum)

    first_peak = jnp.full((head_count, row_count), NEG_FILL, jnp.float32)
    first_total = jnp.zeros((head_count, row_count), jnp.float32)
    first_sum = jnp.zeros((row_count, head_count, head_dim), jnp.float32)
    row_peak, row_total, value_sum = lax.fori_loop(
        0, blocks, online_step, (first_peak, first_total, first_sum)
    )
    log_total = row_peak + jnp.log(row_total)
    output = value_sum / row_total.T[:, :, None]
    return (output.astype(jnp.bfloat16), log_total)


def backprop(
    whole_k,
    whole_v,
    query_rows,
    grad_rows,
    positions,
    log_total,
    row_delta,
    blocks,
    block_width,
    key_acc,
    value_acc,
):
    row_count, head_count, head_dim = query_rows.shape
    score_scale = 1.0 / math.sqrt(head_dim)

    def grad_step(block_index, state_three):
        query_grad, key_sums, value_sums = state_three
        key_start = block_index * block_width
        key_part = lax.dynamic_slice_in_dim(whole_k, key_start, block_width, 0)
        value_part = lax.dynamic_slice_in_dim(whole_v, key_start, block_width, 0)
        scores, visible = block_scores(query_rows, key_part, positions, key_start, score_scale)
        prob_exact = jnp.where(visible, jnp.exp(scores - log_total[:, :, None]), 0.0)
        prob_half = prob_exact.astype(jnp.bfloat16)
        prob_grad = jnp.einsum(
            "nhd,jd->hnj", grad_rows, value_part, preferred_element_type=jnp.float32
        )
        score_grad = (prob_exact * (prob_grad - row_delta[:, :, None]) * score_scale).astype(
            jnp.bfloat16
        )
        query_grad = query_grad + jnp.einsum(
            "hnj,jd->nhd", score_grad, key_part, preferred_element_type=jnp.float32
        )
        key_term = jnp.einsum(
            "hnj,nhd->jd", score_grad, query_rows, preferred_element_type=jnp.float32
        )
        value_term = jnp.einsum(
            "hnj,nhd->jd", prob_half, grad_rows, preferred_element_type=jnp.float32
        )
        old_keys = lax.dynamic_slice_in_dim(key_sums, key_start, block_width, 0)
        old_values = lax.dynamic_slice_in_dim(value_sums, key_start, block_width, 0)
        key_sums = lax.dynamic_update_slice_in_dim(key_sums, old_keys + key_term, key_start, 0)
        value_sums = lax.dynamic_update_slice_in_dim(
            value_sums, old_values + value_term, key_start, 0
        )
        return (query_grad, key_sums, value_sums)

    first_grad = jnp.zeros((row_count, head_count, head_dim), jnp.float32)
    query_grad, key_acc, value_acc = lax.fori_loop(
        0, blocks, grad_step, (first_grad, key_acc, value_acc)
    )
    return (query_grad.astype(jnp.bfloat16), key_acc, value_acc)


def fetch_keys(key_vectors, value_vectors):
    fsdp_size = lax.axis_size("fsdp")
    kv_heads = key_vectors.shape[1] // HD
    repeats = fsdp_size // kv_heads
    rows_k, rows_v = (
        lax.all_gather(key_vectors, "cp", axis=0, tiled=True),
        lax.all_gather(value_vectors, "cp", axis=0, tiled=True),
    )
    gathered_rows = rows_k.shape[0]
    spread_k = jnp.repeat(rows_k.reshape(gathered_rows, kv_heads, HD), repeats, axis=1)
    spread_v = jnp.repeat(rows_v.reshape(gathered_rows, kv_heads, HD), repeats, axis=1)
    got_k, got_v = (
        lax.all_to_all(spread_k, "fsdp", split_axis=1, concat_axis=0, tiled=True),
        lax.all_to_all(spread_v, "fsdp", split_axis=1, concat_axis=0, tiled=True),
    )
    return (got_k.reshape(-1, HD), got_v.reshape(-1, HD))


def per_device(queries, key_vectors, value_vectors, out_grads, pair_order):
    tok_rows = queries.shape[0]
    q_heads = queries.shape[1] // HD
    kv_heads = key_vectors.shape[1] // HD
    half_rows = tok_rows // 2
    cp_size = lax.axis_size("cp")
    fsdp_size = lax.axis_size("fsdp")
    repeats = fsdp_size // kv_heads
    seq_len = tok_rows * cp_size
    block_width = math.gcd(256, seq_len)
    my_index = lax.axis_index("cp")
    first_stretch = pair_order[2 * my_index]
    second_stretch = pair_order[2 * my_index + 1]
    offsets = jnp.arange(tok_rows, dtype=jnp.int32)
    positions = jnp.where(
        offsets < half_rows,
        first_stretch * half_rows + offsets,
        second_stretch * half_rows + offsets - half_rows,
    )
    query_rows = queries.reshape(tok_rows, q_heads, HD)
    grad_rows = out_grads.reshape(tok_rows, q_heads, HD)
    whole_k, whole_v = fetch_keys(key_vectors, value_vectors)
    row_spans = ((0, tok_rows, jnp.maximum(first_stretch, second_stretch) + 1),)
    row_low, row_high, stretch_end = row_spans[0]
    blocks = (stretch_end * half_rows + block_width - 1) // block_width
    span_out, span_log = attend(whole_k, whole_v, query_rows, positions, blocks, block_width)
    row_delta = jnp.sum(grad_rows.astype(jnp.float32) * span_out.astype(jnp.float32), axis=2).T
    whole_k, whole_v = fetch_keys(key_vectors, value_vectors)
    key_acc = jnp.zeros((seq_len, HD), jnp.float32)
    value_acc = jnp.zeros((seq_len, HD), jnp.float32)
    span_grad, key_acc, value_acc = backprop(
        whole_k,
        whole_v,
        query_rows,
        grad_rows,
        positions,
        span_log,
        row_delta,
        blocks,
        block_width,
        key_acc,
        value_acc,
    )
    piece_rows = seq_len // fsdp_size
    term_k = key_acc.reshape(fsdp_size, piece_rows, HD)
    term_v = value_acc.reshape(fsdp_size, piece_rows, HD)
    got_k, got_v = (
        lax.all_to_all(
            term_k.astype(jnp.bfloat16), "fsdp", split_axis=0, concat_axis=0, tiled=True
        ).astype(term_k.dtype),
        lax.all_to_all(
            term_v.astype(jnp.bfloat16), "fsdp", split_axis=0, concat_axis=0, tiled=True
        ).astype(term_v.dtype),
    )
    summed_k = (
        got_k.reshape(kv_heads, repeats, piece_rows, HD)
        .sum(axis=1)
        .transpose(1, 0, 2)
        .reshape(piece_rows, kv_heads * HD)
    )
    summed_v = (
        got_v.reshape(kv_heads, repeats, piece_rows, HD)
        .sum(axis=1)
        .transpose(1, 0, 2)
        .reshape(piece_rows, kv_heads * HD)
    )
    final_k, final_v = (
        lax.psum_scatter(
            summed_k.astype(jnp.bfloat16), "cp", scatter_dimension=0, tiled=True
        ).astype(jnp.float32),
        lax.psum_scatter(
            summed_v.astype(jnp.bfloat16), "cp", scatter_dimension=0, tiled=True
        ).astype(jnp.float32),
    )
    attended = span_out.reshape(tok_rows, q_heads * HD)
    query_grads = span_grad.reshape(tok_rows, q_heads * HD)
    return (attended, query_grads, final_k, final_v)


def solution(mesh):
    return jax.shard_map(
        per_device,
        mesh=mesh,
        in_specs=(
            P("cp", "fsdp"),
            P(("fsdp", "cp"), None),
            P(("fsdp", "cp"), None),
            P("cp", "fsdp"),
            P(),
        ),
        out_specs=(
            P("cp", "fsdp"),
            P("cp", "fsdp"),
            P(("fsdp", "cp"), None),
            P(("fsdp", "cp"), None),
        ),
        check_vma=False,
    )
```

profile of v0, /device:TPU:1, one launch (start us, length us, event | category | flops | bytes accessed | tf_op | source)
XLA Modules:
  0.0 769.2 jit_solution(10527921880946531678)
XLA Ops:
  7.2 53.5 %all_gather.9 = bf16[128,1024]{1,0:T(8,128)(2,1)S(1)} all-gather(bf16[8,1024]{1,0:T(8,128)(2,1)} %param.11), channel_id=1, replica_groups=mesh['fsdp'=32,'cp'=16] {'cp'}, dimensions={0}, use_global_device_ids=true | all-gather | bytes 278528 | tf_op jit(solution)/shard_map/all_gather | solution.py:117
  60.8 1.2 broadcast_in_dim.54
  62.0 14.1 %all-to-all-start.1 = ((bf16[128,32,128]{2,0,1:T(8,128)(2,1)}), bf16[128,32,128]{2,0,1:T(8,128)(2,1)S(1)}, u32[]{:S(2)}, u32[]{:S(2)}) async-start(bf16[128,32,128]{2,0,1:T(8,128)(2,1)} %bitcast.6), calls=%async_computation.1 | async-start | bytes 2097152 | tf_op jit(solution)/shard_map/all_to_all | solution.py:124
  76.1 55.1 %all_gather.8 = bf16[128,1024]{1,0:T(8,128)(2,1)S(1)} all-gather(bf16[8,1024]{1,0:T(8,128)(2,1)S(1)} %copy-done.6), channel_id=1, replica_groups=mesh['fsdp'=32,'cp'=16] {'cp'}, dimensions={0}, use_global_device_ids=true | all-gather | bytes 278528 | tf_op jit(solution)/shard_map/all_gather | solution.py:116
  131.3 1.2 broadcast_in_dim.53
  132.5 15.8 %all-to-all-start = ((bf16[128,32,128]{2,0,1:T(8,128)(2,1)}), bf16[128,32,128]{2,0,1:T(8,128)(2,1)S(1)}, u32[]{:S(2)}, u32[]{:S(2)}) async-start(bf16[128,32,128]{2,0,1:T(8,128)(2,1)} %bitcast.1), calls=%async_computation | async-start | bytes 2097152 | tf_op jit(solution)/shard_map/all_to_all | solution.py:123
  152.2 22.8 %all-to-all-done = bf16[128,32,128]{2,0,1:T(8,128)(2,1)S(1)} async-done(((bf16[128,32,128]{2,0,1:T(8,128)(2,1)}), bf16[128,32,128]{2,0,1:T(8,128)(2,1)S(1)}, u32[]{:S(2)}, u32[]{:S(2)}) %all-to-all-start) | async-done | bytes 1048608 | tf_op jit(solution)/shard_map/all_to_all | solution.py:123
  175.0 12.7 %while.30 = (s32[]{:T(128)}, f32[4,256]{1,0:T(4,128)S(1)}, f32[4,256]{1,0:T(4,128)S(1)}, f32[256,4,128]{0,2,1:T(8,128)S(1)}, s32[]{:T(128)}, /*index=5*/bf16[409...) while((s32[]{:T(128)}, f32[4,256]{1,0:T(4,128)S(1)}, ...), condition=%wide.region_3.4_spmd.clone, body=%wide.region_0.3_spmd.clone.sunk | while | flops 136909312 | bytes 4919495 | solution.py:49
  187.8 0.9 multiply_reduce_fusion
  189.3 1.5 broadcast.77
  190.8 63.3 %while.31 = (s32[]{:T(128)}, f32[256,4,128]{0,2,1:T(8,128)S(1)}, f32[4096,128]{1,0:T(8,128)}, f32[4096,128]{1,0:T(8,128)S(1)}, s32[]{:T(128)}, /*index=5*/bf16[4...) while((s32[]{:T(128)}, f32[256,4,128]{0,2,1:T(8,128)S(1)}, ...), condition=%wide.region_6.7_spmd.clone, body=%wide.region_5.6_spmd.clone.sunk | while | flops 337905152 | bytes 7680235 | solution.py:105
  190.9 1.2 fusion.94
  192.2 1.1 fusion.95
  193.3 1.1 fusion.96
  194.7 1.8 fusion.97
  196.7 1.2 fusion.94
  197.9 1.1 fusion.95
  199.1 1.1 fusion.96
  200.5 1.9 fusion.97
  202.5 1.2 fusion.94
  203.7 1.1 fusion.95
  204.8 1.1 fusion.96
  206.2 1.8 fusion.97
  208.2 1.2 fusion.94
  209.4 1.1 fusion.95
  210.6 1.1 fusion.96
  212.0 1.8 fusion.97
  214.0 1.2 fusion.94
  215.2 1.1 fusion.95
  216.3 1.1 fusion.96
  217.7 1.8 fusion.97
  219.7 1.2 fusion.94
  220.9 1.1 fusion.95
  222.1 1.1 fusion.96
  223.5 1.8 fusion.97
  225.5 1.2 fusion.94
  226.7 1.1 fusion.95
  227.8 1.1 fusion.96
  229.2 1.8 fusion.97
  231.2 1.2 fusion.94
  232.4 1.1 fusion.95
  233.6 1.1 fusion.96
  235.0 1.8 fusion.97
  237.0 1.2 fusion.94
  238.2 1.1 fusion.95
  239.3 1.1 fusion.96
  240.8 1.9 fusion.97
  242.7 1.2 fusion.94
  244.0 1.1 fusion.95
  245.1 1.1 fusion.96
  246.5 1.8 fusion.97
  248.5 1.2 fusion.94
  249.7 1.1 fusion.95
  250.9 1.1 fusion.96
  252.3 1.8 fusion.97
  254.1 1.1 convert_element_type.69
  255.2 5.3 all-to-all-start.3
  260.5 1.1 convert_element_type.63
  261.6 25.6 %all-to-all-done.3 = bf16[32,128,128]{2,1,0:T(8,128)(2,1)} async-done(((bf16[32,128,128]{2,1,0:T(8,128)(2,1)}), bf16[32,128,128]{2,1,0:T(8,128)(2,1)}, u32[]{:S(2)}, u32[]{:S(2)}) %all-to-all-start.3) | async-done | bytes 1048608 | tf_op jit(solution)/shard_map/all_to_all | solution.py:179
  287.2 5.1 all-to-all-start.2
  292.4 1.4 bitcast_reduce_fusion
  294.9 24.1 %all-to-all-done.2 = bf16[32,128,128]{2,1,0:T(8,128)(2,1)S(1)} async-done(((bf16[32,128,128]{2,1,0:T(8,128)(2,1)}), bf16[32,128,128]{2,1,0:T(8,128)(2,1)S(1)}, u32[]{:S(2)}, u32[]{:S(2)}) %all-to-all-start.2) | async-done | bytes 1048608 | tf_op jit(solution)/shard_map/all_to_all | solution.py:176
  321.9 218.8 %reduce-scatter.9.cloned.1.call-done = bf16[8,1024]{1,0:T(8,128)(2,1)} async-done(((bf16[128,1024]{1,0:T(8,128)(2,1)}), bf16[8,1024]{1,0:T(8,128)(2,1)}) %reduce-scatter.9.cloned.1.call-update) | async-done | bytes 16400
  542.3 218.4 %reduce-scatter.7.cloned.1.call-done = bf16[8,1024]{1,0:T(8,128)(2,1)} async-done(((bf16[128,1024]{1,0:T(8,128)(2,1)}), bf16[8,1024]{1,0:T(8,128)(2,1)}) %reduce-scatter.7.cloned.1.call-update) | async-done | bytes 16400
  (167 shorter events, 25.7 us)
Async XLA Ops:
  7.2 68.9 %copy-start.6 = (bf16[8,1024]{1,0:T(8,128)(2,1)S(1)}, bf16[8,1024]{1,0:T(8,128)(2,1)}, u32[]{:S(2)}) copy-start(bf16[8,1024]{1,0:T(8,128)(2,1)} %param.10) | copy-start | bytes 49156
  62.0 69.3 %all-to-all-start.1 = ((bf16[128,32,128]{2,0,1:T(8,128)(2,1)}), bf16[128,32,128]{2,0,1:T(8,128)(2,1)S(1)}, u32[]{:S(2)}, u32[]{:S(2)}) async-start(bf16[128,32,128]{2,0,1:T(8,128)(2,1)} %bitcast.6), calls=%async_computation.1 | async-start | bytes 2097152 | tf_op jit(solution)/shard_map/all_to_all | solution.py:124
  76.1 72.2 %copy-start.7 = (s32[32]{0:T(128)S(1)}, s32[32]{0:T(128)}, u32[]{:S(2)}) copy-start(s32[32]{0:T(128)} %param.13) | copy-start | bytes 388
  76.1 75.4 %copy-start.4 = (bf16[256,512]{1,0:T(8,128)(2,1)S(1)}, bf16[256,512]{1,0:T(8,128)(2,1)}, u32[]{:S(2)}) copy-start(bf16[256,512]{1,0:T(8,128)(2,1)} %param.12) | copy-start | bytes 786436
  131.3 20.5 %copy-start.5 = (bf16[256,512]{1,0:T(8,128)(2,1)S(1)}, bf16[256,512]{1,0:T(8,128)(2,1)}, u32[]{:S(2)}) copy-start(bf16[256,512]{1,0:T(8,128)(2,1)} %param.9) | copy-start | bytes 786436
  132.5 42.4 %all-to-all-start = ((bf16[128,32,128]{2,0,1:T(8,128)(2,1)}), bf16[128,32,128]{2,0,1:T(8,128)(2,1)S(1)}, u32[]{:S(2)}, u32[]{:S(2)}) async-start(bf16[128,32,128]{2,0,1:T(8,128)(2,1)} %bitcast.1), calls=%async_computation | async-start | bytes 2097152 | tf_op jit(solution)/shard_map/all_to_all | solution.py:123
  187.7 1.1 copy-start.1
  187.7 1.4 copy-start.2
  255.2 5.3 copy-start
  255.2 32.0 %all-to-all-start.3 = ((bf16[32,128,128]{2,1,0:T(8,128)(2,1)}), bf16[32,128,128]{2,1,0:T(8,128)(2,1)}, u32[]{:S(2)}, u32[]{:S(2)}) async-start(bf16[32,128,128]{2,1,0:T(8,128)(2,1)} %bitcast.152), calls=%async_computation.3 | async-start | bytes 2097152 | tf_op jit(solution)/shard_map/all_to_all | solution.py:179
  287.2 31.8 %all-to-all-start.2 = ((bf16[32,128,128]{2,1,0:T(8,128)(2,1)}), bf16[32,128,128]{2,1,0:T(8,128)(2,1)S(1)}, u32[]{:S(2)}, u32[]{:S(2)}) async-start(bf16[32,128,128]{2,1,0:T(8,128)(2,1)} %bitcast.151), calls=%async_computation.2 | async-start | bytes 2097152 | tf_op jit(solution)/shard_map/all_to_all | solution.py:176
  292.3 248.4 %reduce-scatter.9.cloned.1.call-start = ((), (), s32[]{:S(2)}) async-start(), calls=%async_computation.7 | async-start | bytes 278528
  293.7 26.4 %copy-start.3 = (bf16[256,4,128]{0,2,1:T(8,128)(2,1)S(1)}, bf16[256,4,128]{0,2,1:T(8,128)(2,1)}, u32[]{:S(2)}) copy-start(bf16[256,4,128]{0,2,1:T(8,128)(2,1)} %get-tuple-element.348) | copy-start | bytes 786436
  294.8 465.9 %reduce-scatter.7.cloned.1.call-start = ((), (), s32[]{:S(2)}) async-start(), calls=%async_computation.6 | async-start | bytes 278528
Sparse Core Ops, SparseCore 0:
  297.6 243.0 reduce-scatter.8
  545.1 215.5 reduce-scatter.6
where the time goes:
time: 775 us; the launch traced here: 769 us
  waiting for transfers between devices  510 us (66%)
  blocking collectives  109 us (14%)
  matrix products  69.9 us (9%)
  starting transfers between devices  40.4 us (5%)
  between operations  16.9 us (2%)
  local copies, waits for them, and re-layouts  12.9 us (2%)
  other arithmetic  9.67 us (1%)
    unnamed x4, waiting for transfers between devices  437 us
    all_gather x1, blocking collectives, fetch_keys(): lax.all_gather(key_vectors, 'cp', axis=0, tiled=True)  55.1 us
    all_gather x1, blocking collectives, fetch_keys(): lax.all_gather(value_vectors, 'cp', axis=0, tiled=True)  53.5 us
    all_to_all x1, waiting for transfers between devices, per_device(): lax.all_to_all(term_v.astype(jnp.bfloat16), 'fsdp', split_axis=0, concat_...  25.6 us
    all_to_all x1, waiting for transfers between devices, per_device(): lax.all_to_all(term_k.astype(jnp.bfloat16), 'fsdp', split_axis=0, concat_...  24.1 us
    all_to_all x1, waiting for transfers between devices, fetch_keys(): lax.all_to_all(spread_k, 'fsdp', split_axis=1, concat_axis=0, tiled=True)  22.8 us
    dot_general x11, matrix products, grad_step(): jnp.einsum('hnj,nhd->jd', score_grad, query_rows, preferred_element_type=...  20.3 us
    dot_general x22, matrix products, block_scores(): jnp.einsum('nhd,jd->hnj', query_rows, key_part, preferred_element_type=jn...  17 us
  transfers between devices with their start and end apart: 6, of which 5 were waited for; matrix products, arithmetic and copies ran while one was open for 1% of the time, Pallas kernels for 0%

commit v1 on v0

v1 whole, which is shorter than its diff:
```python
import math
import jax
import jax.numpy as jnp
from jax import lax
from jax.experimental import pallas as pl
from jax.experimental.pallas import tpu as pltpu
from jax.sharding import Mesh, PartitionSpec as P

HD = 128
BF16 = jnp.bfloat16
F32 = jnp.float32


def nn(a, b):
    return jnp.dot(a, b, preferred_element_type=F32)


def tn(a, b):
    return lax.dot_general(a, b, (((0,), (0,)), ((), ())), preferred_element_type=F32)


def flip(x):
    return x.astype(F32).T


def attention_kernel(
    order_ref,
    q_ref,
    g_ref,
    mine_ref,
    theirs_ref,
    out_ref,
    dq_ref,
    dmine_ref,
    dtheirs_ref,
    s_ref,
    e_ref,
    qn_ref,
    qt_ref,
    gn_ref,
    gt_ref,
    acc_ref,
    delta_ref,
):
    half = q_ref.shape[0] // 2
    heads = q_ref.shape[1] // HD
    cols = heads * half
    runs, pairs, _, grain, _ = mine_ref.shape
    scale = 1.0 / math.sqrt(HD)
    rate = scale * math.log2(math.e)
    core = lax.axis_index("core")
    first = 2 * (lax.axis_index("y") * lax.axis_size("zh") + lax.axis_index("zh"))
    late = jnp.where(order_ref[first + 1] > order_ref[first], 1, 0)
    stretches = (order_ref[first + late], order_ref[first + 1 - late])
    offsets = (
        pl.multiple_of(late * half, half),
        pl.multiple_of((1 - late) * half, half),
    )
    counts = tuple(lax.shift_right_logical(s, 1) + 1 for s in stretches)

    def rows_of(index, which):
        parts = (mine_ref[:, index, which], theirs_ref[:, index, which])
        return jnp.concatenate([p.reshape(half, HD) for p in parts], axis=0)

    for t in range(2):
        for h in range(heads):
            span = slice(t * cols + h * half, t * cols + (h + 1) * half)
            block = q_ref[pl.ds(offsets[t], half), h * HD : (h + 1) * HD]
            qn_ref[span, :] = block
            qt_ref[:, span] = flip(block).astype(BF16)

    for t in range(2):
        span = slice(t * cols, (t + 1) * cols)
        base = 0 if t == 0 else pairs

        def score(index, peak, masked):
            s = nn(rows_of(index, 0), qt_ref[:, span])
            if masked:
                j = lax.broadcasted_iota(jnp.int32, s.shape, 0)
                r = lax.broadcasted_iota(jnp.int32, s.shape, 1)
                shift = jnp.where(j < half, core * half, -core * half)
                row = lax.rem(r, half) + lax.rem(stretches[t], 2) * half
                s = jnp.where(j + shift <= row, s, -1e30)
            s_ref[index] = s
            return jnp.maximum(peak, jnp.max(s.reshape(-1, 8, cols), axis=0))

        last = counts[t] - 1
        peak = jnp.full((8, cols), -1e30, F32)
        peak = lax.fori_loop(0, last, lambda i, p: score(i, p, False), peak)
        peak = score(last, peak, True)
        shift = jnp.max(peak, axis=0, keepdims=True) * rate

        acc_ref[t] = jnp.zeros((HD, cols), F32)

        def weigh(index, total):
            e = jnp.exp2(s_ref[index] * rate - shift)
            total = total + jnp.sum(e.reshape(-1, 8, cols), axis=0)
            weight = e.astype(BF16)
            e_ref[base + index] = weight
            acc_ref[t] += tn(rows_of(index, 1), weight)
            return total

        total = lax.fori_loop(0, counts[t], weigh, jnp.zeros((8, cols), F32))
        inverse = 1.0 / jnp.sum(total, axis=0, keepdims=True)
        for h in range(heads):
            part = slice(h * half, (h + 1) * half)
            full = slice(t * cols + h * half, t * cols + (h + 1) * half)
            column = slice(h * HD, (h + 1) * HD)
            out = (acc_ref[t, :, part] * inverse[:, part]).astype(BF16)
            out_ref[pl.ds(offsets[t], half), column] = flip(out).astype(BF16)
            grad = flip(g_ref[pl.ds(offsets[t], half), column]) * inverse[:, part]
            half_grad = grad.astype(BF16)
            gt_ref[:, full] = half_grad
            gn_ref[full, :] = flip(half_grad).astype(BF16)
            delta = jnp.sum(grad * out.astype(F32), axis=0, keepdims=True)
            delta_ref[t, :, part] = delta
        acc_ref[t] = jnp.zeros((HD, cols), F32)

    def store(index, which, value):
        value = value.astype(BF16)
        shape = (runs, grain, HD)
        dmine_ref[:, index, which] = value[:half].reshape(shape)
        dtheirs_ref[:, index, which] = value[half:].reshape(shape)

    def pull(index, both):
        keys = rows_of(index, 0)
        values = rows_of(index, 1)
        key_term = jnp.zeros((2 * half, HD), F32)
        value_term = jnp.zeros((2 * half, HD), F32)
        for t in range(2 if both else 1):
            span = slice(t * cols, (t + 1) * cols)
            weight = e_ref[index if t == 0 else pairs + index]
            slope = nn(values, gt_ref[:, span]) - delta_ref[t]
            ds = (weight.astype(F32) * slope).astype(BF16)
            value_term = value_term + nn(weight, gn_ref[span, :])
            key_term = key_term + nn(ds, qn_ref[span, :])
            acc_ref[t] += tn(keys, ds)
        store(index, 0, key_term * scale)
        store(index, 1, value_term)

    @pl.loop(0, counts[1])
    def _(index):
        pull(index, True)

    @pl.loop(counts[1], counts[0])
    def _(index):
        pull(index, False)

    @pl.loop(counts[0], pairs)
    def _(index):
        for which in range(2):
            store(index, which, jnp.zeros((2 * half, HD), F32))

    for t in range(2):
        for h in range(heads):
            part = slice(h * half, (h + 1) * half)
            value = (acc_ref[t, :, part] * scale).T.astype(BF16)
            dq_ref[pl.ds(offsets[t], half), h * HD : (h + 1) * HD] = value


def attention(order, queries, grads, mine, theirs):
    rows, width = queries.shape
    half, cols, pairs = rows // 2, width // HD * (rows // 2), mine.shape[1]
    vmem = pl.BlockSpec(memory_space=pltpu.VMEM)
    return pl.pallas_call(
        attention_kernel,
        out_shape=(
            jax.ShapeDtypeStruct(queries.shape, BF16),
            jax.ShapeDtypeStruct(queries.shape, BF16),
            jax.ShapeDtypeStruct(mine.shape, BF16),
            jax.ShapeDtypeStruct(mine.shape, BF16),
        ),
        in_specs=[pl.BlockSpec(memory_space=pltpu.SMEM)] + [vmem] * 4,
        out_specs=(vmem,) * 4,
        scratch_shapes=[
            pltpu.VMEM((pairs, 2 * half, cols), F32),
            pltpu.VMEM((pairs + pairs // 2, 2 * half, cols), BF16),
            pltpu.VMEM((2 * cols, HD), BF16),
            pltpu.VMEM((HD, 2 * cols), BF16),
            pltpu.VMEM((2 * cols, HD), BF16),
            pltpu.VMEM((HD, 2 * cols), BF16),
            pltpu.VMEM((2, HD, cols), F32),
            pltpu.VMEM((2, 1, cols), F32),
        ],
        compiler_params=pltpu.CompilerParams(vmem_limit_bytes=48 << 20),
        name="attention",
    )(order, queries, grads, mine, theirs)


AXES = ("zl", "xh", "xl", "core", "y", "zh")
SPREAD = ("zl", "xh", "xl", "zh")
SWAP = ((0, 1), (1, 0))


def per_device(queries, key_vectors, value_vectors, out_grads, pair_order):
    sizes = {name: lax.axis_size(name) for name in AXES}
    zl, xh, xl, zh = (sizes[name] for name in SPREAD)
    rows = key_vectors.shape[0]
    kv_heads = key_vectors.shape[1] // HD
    runs = sizes["y"]
    pairs = zl * xh * xl

    both = jnp.stack([key_vectors, value_vectors]).reshape(2, rows, kv_heads, HD)
    sent = both.transpose(2, 0, 1, 3).reshape(zl, xh, 1, 1, 2, rows, HD)
    sent = jnp.broadcast_to(sent, (zl, xh, xl, zh, 2, rows, HD))
    sent = sent.reshape(pairs * zh, 2, rows, HD)
    got = lax.all_to_all(sent, SPREAD, split_axis=0, concat_axis=0, tiled=True)
    run = got.reshape(pairs, zh, 2, rows, HD).transpose(0, 2, 1, 3, 4)
    run = run.reshape(1, pairs, 2, zh * rows, HD)
    whole = jnp.broadcast_to(run, (runs,) + run.shape[1:])
    mine = lax.all_to_all(whole, "y", split_axis=0, concat_axis=0, tiled=True)
    theirs = lax.ppermute(mine, "core", SWAP)

    attended, query_grads, dmine, dtheirs = attention(
        pair_order, queries, out_grads, mine, theirs
    )

    other = lax.ppermute(dtheirs, "core", SWAP)
    total = (dmine.astype(F32) + other.astype(F32)).astype(BF16)
    got = lax.all_to_all(total, "y", split_axis=0, concat_axis=0, tiled=True)
    total = got.astype(F32).sum(axis=0).astype(BF16)
    total = total.reshape(pairs, 2, zh, rows, HD).transpose(0, 2, 1, 3, 4)
    total = total.reshape(pairs * zh, 2, rows, HD)
    got = lax.all_to_all(total, SPREAD, split_axis=0, concat_axis=0, tiled=True)
    total = got.reshape(kv_heads, xl * zh, 2, rows, HD).astype(F32).sum(axis=1)
    total = total.transpose(1, 2, 0, 3).reshape(2, rows, kv_heads * HD)
    return attended, query_grads, total[0], total[1]


def solution(mesh):
    fine = Mesh(mesh.devices.reshape(4, 2, 2, 2, 8, 2), AXES)
    fsdp, cp = AXES[:4], AXES[4:]
    return jax.shard_map(
        per_device,
        mesh=fine,
        in_specs=(P(cp, fsdp), P(AXES, None), P(AXES, None), P(cp, fsdp), P()),
        out_specs=(P(cp, fsdp), P(cp, fsdp), P(AXES, None), P(AXES, None)),
        check_vma=False,
    )
```

time: 775 us -> 132 us (0.17)
  waiting for transfers between devices: 510 us -> 4.53 us
  matrix products: 69.9 us -> 0 us
  starting transfers between devices: 40.4 us -> 8.07 us
  Pallas kernels: 0 us -> 16.9 us
  between operations: 16.9 us -> 0.73 us
  local copies, waits for them, and re-layouts: 12.9 us -> 0.89 us
  blocking collectives: 109 us -> 99.4 us
  other arithmetic: 9.67 us -> 1.22 us
    unnamed x4 -> x0, waiting for transfers between devices: 437 us -> none
    all_gather x2 -> x0, blocking collectives: 109 us -> none  [the longest x1 55.1 us: fetch_keys(): lax.all_gather(key_vectors, 'cp', axis=0, tiled=True)]
    all_to_all x0 -> x4, blocking collectives: none -> 99.4 us  [the longest x1 32.6 us: per_device(): mine = lax.all_to_all(whole, 'y', split_axis=0, concat_axis=0, tiled=True)]
    all_to_all x4 -> x0, waiting for transfers between devices: 72.5 us -> none  [the longest x1 25.6 us: per_device(): lax.all_to_all(term_v.astype(jnp.bfloat16), 'fsdp', split_axis=0, concat_...]
    dot_general x77 -> x0, matrix products: 69.9 us -> none  [the longest x11 20.3 us: grad_step(): jnp.einsum('hnj,nhd->jd', score_grad, query_rows, preferred_element_type=...]
    all_to_all x4 -> x0, starting transfers between devices: 40.3 us -> none  [the longest x1 15.8 us: fetch_keys(): lax.all_to_all(spread_k, 'fsdp', split_axis=1, concat_axis=0, tiled=True)]
    pallas_call x0 -> x1, Pallas kernels: none -> 16.9 us  [attention(): pl.pallas_call(attention_kernel, out_shape=(jax.ShapeDtypeStruct(queries....]
    ppermute x0 -> x2, starting transfers between devices: none -> 8.07 us  [the longest x1 5.77 us: per_device(): theirs = lax.ppermute(mine, 'core', SWAP)]
  transfers between devices with their start and end apart: 6 -> 2, of which waited for: 5 -> 2; matrix products, arithmetic and copies ran while one was open for 1% -> 0% of each run, Pallas kernels for 0% -> 0%
where the time goes in v1:
time: 132 us
  blocking collectives  99.4 us (75%)
  Pallas kernels  16.9 us (13%)
  starting transfers between devices  8.07 us (6%)
  waiting for transfers between devices  4.53 us (3%)
    all_to_all x1, blocking collectives, per_device(): mine = lax.all_to_all(whole, 'y', split_axis=0, concat_axis=0, tiled=True)  32.6 us
    all_to_all x1, blocking collectives, per_device(): got = lax.all_to_all(total, 'y', split_axis=0, concat_axis=0, tiled=True)  31.6 us
    all_to_all x1, blocking collectives, per_device(): got = lax.all_to_all(sent, SPREAD, split_axis=0, concat_axis=0, tiled=True)  22.6 us
    pallas_call x1, Pallas kernels, attention(): pl.pallas_call(attention_kernel, out_shape=(jax.ShapeDtypeStruct(queries....  16.9 us
    all_to_all x1, blocking collectives, per_device(): got = lax.all_to_all(total, SPREAD, split_axis=0, concat_axis=0, tiled=True)  12.6 us
    ppermute x1, starting transfers between devices, per_device(): theirs = lax.ppermute(mine, 'core', SWAP)  5.77 us
  transfers between devices with their start and end apart: 2, of which 2 were waited for; matrix products, arithmetic and copies ran while one was open for 0% of the time, Pallas kernels for 0%

profile of v1, /device:TPU:1, one launch (start us, length us, event | category | flops | bytes accessed | tf_op | source)
XLA Modules:
  0.0 131.8 jit_solution(18206183134050826303)
XLA Ops:
  0.6 0.7 pad_maximum_fusion.1
  1.4 22.6 %all_to_all.20 = bf16[32,2,8,128]{3,2,1,0:T(8,128)(2,1)S(1)} all-to-all(bf16[32,2,8,128]{3,2,1,0:T(8,128)(2,1)S(1)} %bitcast.22), channel_id=1, replica_groups=mesh['zl'=4,'xh'=2,'xl'=2,'core'=2,'y'=8,'zh'=2] {'zl','xh','xl','zh'}, dimensions={0} | all-to-all | bytes 262144 | tf_op jit(solution)/shard_map/all_to_all | solution.py:207
  24.1 0.2 broadcast_in_dim.17
  24.2 0.0 copy-start
  24.3 0.0 copy-start.1
  24.3 0.0 copy-start.2
  24.3 32.6 %all_to_all.21.mine_ref = bf16[8,16,2,16,128]{4,3,2,1,0:T(8,128)(2,1)S(1)} all-to-all(bf16[8,16,2,16,128]{4,3,2,1,0:T(8,128)(2,1)S(1)} %broadcast_in_dim.17), channel_id=1, replica_groups=mesh['zl'=4,'xh'=2,'xl'=2,'core'=2,'y'=8,'zh'=2] {'y'}, dimensions={0} | all-to-all | bytes 2097152 | tf_op jit(solution)/shard_map/all_to_all | solution.py:211
  56.8 5.8 %collective-permute-start = (bf16[8,16,2,16,128]{4,3,2,1,0:T(8,128)(2,1)S(1)}, bf16[8,16,2,16,128]{4,3,2,1,0:T(8,128)(2,1)S(1)}, u32[]{:S(2)}, u32[]{:S(2)}) collective-permute-start(bf16[8,16,2,16,128]{4,3,2,1,0:T(8,128)(2,1)S(1)} %all_to_all.21.mine_ref), channel_id=1, source_target_pairs={{0,16},{16,0},{1,17},{17,1},{2,18},{18,2},{3,19},{19,3},{4,20},{20... | collective-permute-start | bytes 3145736 | tf_op jit(solution)/shard_map/ppermute | solution.py:212
  62.6 2.3 %collective-permute-done.theirs_ref = bf16[8,16,2,16,128]{4,3,2,1,0:T(8,128)(2,1)S(1)} collective-permute-done((bf16[8,16,2,16,128]{4,3,2,1,0:T(8,128)(2,1)S(1)}, bf16[8,16,2,16,128]{4,3,2,1,0:T(8,128)(2,1)S(1)}, u32[]{:S(2)}, u32[]{:S(2)}) %collective-permute-start) | collective-permute-done | bytes 1048608 | tf_op jit(solution)/shard_map/ppermute | solution.py:212
  64.9 0.0 copy-done
  64.9 0.0 copy-done.1
  64.9 0.0 copy-done.2
  64.9 16.9 %attention.1 = (bf16[256,512]{1,0:T(8,128)(2,1)}, bf16[256,512]{1,0:T(8,128)(2,1)}, bf16[8,16,2,16,128]{4,3,2,1,0:T(8,128)(2,1)S(1)}, bf16[8,16,2,16,128]{4,3,2,1,0:T(8,128)(2,1)S(1)}) custom-call(s32[32]{0:T(128)S(1)} %copy-done.2, bf16[256,512]{1,0:T(8,128)(2,1)S(1)} %copy-done, bf16[256,512]{1,0:T(8,128)(2,1)S(1)} %copy-done.1, ...), custom_call_target="tpu_custom_call" | custom-call | tf_op jit(solution)/shard_map/attention/pallas_call | solution.py:165
  81.8 2.3 %collective-permute-start.1 = (bf16[8,16,2,16,128]{4,3,2,1,0:T(8,128)(2,1)S(1)}, bf16[8,16,2,16,128]{4,3,2,1,0:T(8,128)(2,1)S(1)}, u32[]{:S(2)}, u32[]{:S(2)}) collective-permute-start(bf16[8,16,2,16,128]{4,3,2,1,0:T(8,128)(2,1)S(1)} %get-tuple-element.11), channel_id=1, source_target_pairs={{0,16},{16,0},{1,17},{17,1},{2,18},{18,2},{3,19},{19,3},{4,20},{20... | collective-permute-start | bytes 3145736 | tf_op jit(solution)/shard_map/ppermute | solution.py:218
  84.1 2.3 %collective-permute-done.1 = bf16[8,16,2,16,128]{4,3,2,1,0:T(8,128)(2,1)S(1)} collective-permute-done((bf16[8,16,2,16,128]{4,3,2,1,0:T(8,128)(2,1)S(1)}, bf16[8,16,2,16,128]{4,3,2,1,0:T(8,128)(2,1)S(1)}, u32[]{:S(2)}, u32[]{:S(2)}) %collective-permute-start.1) | collective-permute-done | bytes 1048608 | tf_op jit(solution)/shard_map/ppermute | solution.py:218
  86.4 0.3 add_convert_fusion
  86.7 31.6 %all_to_all.22 = bf16[8,16,2,16,128]{4,3,2,1,0:T(8,128)(2,1)S(1)} all-to-all(bf16[8,16,2,16,128]{4,3,2,1,0:T(8,128)(2,1)S(1)} %add_convert_fusion), channel_id=1, replica_groups=mesh['zl'=4,'xh'=2,'xl'=2,'core'=2,'y'=8,'zh'=2] {'y'}, dimensions={0} | all-to-all | bytes 2097152 | tf_op jit(solution)/shard_map/all_to_all | solution.py:220
  118.3 0.1 reduce_sum.21
  118.5 12.6 %all_to_all.23 = bf16[32,2,8,128]{3,2,1,0:T(8,128)(2,1)S(1)} all-to-all(bf16[32,2,8,128]{3,2,1,0:T(8,128)(2,1)S(1)} %bitcast.23), channel_id=1, replica_groups=mesh['zl'=4,'xh'=2,'xl'=2,'core'=2,'y'=8,'zh'=2] {'zl','xh','xl','zh'}, dimensions={0} | all-to-all | bytes 262144 | tf_op jit(solution)/shard_map/all_to_all | solution.py:224
  131.1 0.6 slice_bitcast_fusion
  (6 shorter events, 0.1 us)
Async XLA Ops:
  24.2 40.6 %copy-start = (bf16[256,512]{1,0:T(8,128)(2,1)S(1)}, bf16[256,512]{1,0:T(8,128)(2,1)}, u32[]{:S(2)}) copy-start(bf16[256,512]{1,0:T(8,128)(2,1)} %q_ref.1) | copy-start | bytes 786436
  24.3 40.6 %copy-start.1 = (bf16[256,512]{1,0:T(8,128)(2,1)S(1)}, bf16[256,512]{1,0:T(8,128)(2,1)}, u32[]{:S(2)}) copy-start(bf16[256,512]{1,0:T(8,128)(2,1)} %g_ref.1) | copy-start | bytes 786436
  24.3 40.6 %copy-start.2 = (s32[32]{0:T(128)S(1)}, s32[32]{0:T(128)}, u32[]{:S(2)}) copy-start(s32[32]{0:T(128)} %order_ref.1) | copy-start | bytes 388
  56.8 8.0 %collective-permute-start = (bf16[8,16,2,16,128]{4,3,2,1,0:T(8,128)(2,1)S(1)}, bf16[8,16,2,16,128]{4,3,2,1,0:T(8,128)(2,1)S(1)}, u32[]{:S(2)}, u32[]{:S(2)}) collective-permute-start(bf16[8,16,2,16,128]{4,3,2,1,0:T(8,128)(2,1)S(1)} %all_to_all.21.mine_ref), channel_id=1, source_target_pairs={{0,16},{16,0},{1,17},{17,1},{2,18},{18,2},{3,19},{19,3},{4,20},{20... | collective-permute-start | bytes 3145736 | tf_op jit(solution)/shard_map/ppermute | solution.py:212
  81.8 4.6 %collective-permute-start.1 = (bf16[8,16,2,16,128]{4,3,2,1,0:T(8,128)(2,1)S(1)}, bf16[8,16,2,16,128]{4,3,2,1,0:T(8,128)(2,1)S(1)}, u32[]{:S(2)}, u32[]{:S(2)}) collective-permute-start(bf16[8,16,2,16,128]{4,3,2,1,0:T(8,128)(2,1)S(1)} %get-tuple-element.11), channel_id=1, source_target_pairs={{0,16},{16,0},{1,17},{17,1},{2,18},{18,2},{3,19},{19,3},{4,20},{20... | collective-permute-start | bytes 3145736 | tf_op jit(solution)/shard_map/ppermute | solution.py:218

commit v2 on v1

v2 whole, which is shorter than its diff:
```python
import math
import jax
import jax.numpy as jnp
from jax import lax
from jax.experimental import pallas as pl
from jax.experimental.pallas import tpu as pltpu
from jax.sharding import Mesh, PartitionSpec as P

HD = 128
BF16 = jnp.bfloat16
F32 = jnp.float32
SCALE = 1.0 / math.sqrt(HD)
RATE = SCALE * math.log2(math.e)
FILL = -1e30
VMEM_BYTES = 32 << 20


def dot(a, b, a_axis, b_axis):
    return lax.dot_general(
        a, b, (((a_axis,), (b_axis,)), ((), ())), preferred_element_type=F32
    )


def flip(x):
    return x.astype(F32).T


def stretches_of(order_ref, half):
    first = 2 * (lax.axis_index("y") * lax.axis_size("zh") + lax.axis_index("zh"))
    late = jnp.where(order_ref[first + 1] > order_ref[first], 1, 0)
    stretches = (order_ref[first + late], order_ref[first + 1 - late])
    offsets = (
        pl.multiple_of(late * half, half),
        pl.multiple_of((1 - late) * half, half),
    )
    return stretches, offsets


def counts_of(stretches, parity):
    seen = [lax.shift_right_logical(s - parity + 2, 1) for s in stretches]
    return tuple(jnp.maximum(lax.shift_right_logical(n + 1, 1), 1) for n in seen)


def block_of(ref, index, which):
    runs, _, _, grain, _ = ref.shape
    parts = [ref[:, 2 * index + u, which].reshape(runs * grain, HD) for u in range(2)]
    return jnp.concatenate(parts, axis=0)


def forward(keys_ref, parity, stretches, qt_ref, s_ref, e_ref, acc_ref):
    cols = s_ref.shape[2]
    blocks = keys_ref.shape[1] // 2
    half = s_ref.shape[1] // 2
    counts = counts_of(stretches, parity)
    bases = (0, blocks)
    shifts = []
    for t in range(2):
        span = slice(t * cols, (t + 1) * cols)

        def score(index, peak, masked):
            s = dot(block_of(keys_ref, index, 0), qt_ref[:, span], 1, 0)
            if masked:
                j = lax.broadcasted_iota(jnp.int32, s.shape, 0)
                r = lax.rem(lax.broadcasted_iota(jnp.int32, s.shape, 1), half)
                j = j + jnp.where(j >= half, half, 0)
                ahead = (4 * index + parity - stretches[t]) * half
                s = jnp.where(j + ahead <= r, s, FILL)
            s_ref[bases[t] + index] = s
            return jnp.maximum(peak, jnp.max(s.reshape(-1, 8, cols), axis=0))

        last = counts[t] - 1
        peak = jnp.full((8, cols), FILL, F32)
        peak = lax.fori_loop(0, last, lambda i, p: score(i, p, False), peak)
        peak = score(last, peak, True)
        shifts.append(jnp.max(peak, axis=0, keepdims=True) * RATE)

    results = []
    for t in range(2):

        def weigh(index, total):
            e = jnp.exp2(s_ref[bases[t] + index] * RATE - shifts[t])
            e_ref[bases[t] + index] = e.astype(BF16)
            return total + jnp.sum(e.reshape(-1, 8, cols), axis=0)

        def attend(index):
            return dot(block_of(keys_ref, index, 1), e_ref[bases[t] + index], 0, 0)

        def step(index, total):
            acc_ref[t] += attend(index - 1)
            return weigh(index, total)

        acc_ref[t] = jnp.zeros(acc_ref.shape[1:], F32)
        total = weigh(0, jnp.zeros((8, cols), F32))
        total = lax.fori_loop(1, counts[t], step, total)
        acc_ref[t] += attend(counts[t] - 1)
        results.append((shifts[t], jnp.sum(total, axis=0, keepdims=True)))
    return results


def backward(keys_ref, parity, stretches, qt_ref, gt_ref, delta_ref, e_ref, acc_ref, out_ref):
    runs, pairs, _, grain, _ = keys_ref.shape
    cols = qt_ref.shape[1] // 2
    half = runs * grain
    blocks = pairs // 2
    counts = counts_of(stretches, parity)

    def store(index, which, value):
        for u in range(2):
            part = value[u * half : (u + 1) * half].reshape(runs, grain, HD)
            out_ref[:, 2 * index + u, which] = part

    def pull(index, both):
        keys = block_of(keys_ref, index, 0)
        values = block_of(keys_ref, index, 1)
        key_term = value_term = None
        for t in range(2 if both else 1):
            span = slice(t * cols, (t + 1) * cols)
            weight = e_ref[index if t == 0 else blocks + index]
            slope = dot(values, gt_ref[:, span], 1, 0) - delta_ref[t]
            ds = (weight.astype(F32) * slope).astype(BF16)
            acc_ref[t] += dot(keys, ds, 0, 0)
            value_part = dot(gt_ref[:, span], weight, 1, 1)
            key_part = dot(qt_ref[:, span], ds, 1, 1)
            value_term = value_part if t == 0 else value_term + value_part
            key_term = key_part if t == 0 else key_term + key_part
        store(index, 0, (key_term * SCALE).T.astype(BF16))
        store(index, 1, value_term.T.astype(BF16))

    @pl.loop(0, counts[1])
    def _(index):
        pull(index, True)

    @pl.loop(counts[1], counts[0])
    def _(index):
        pull(index, False)

    @pl.loop(counts[0], blocks)
    def _(index):
        for which in range(2):
            store(index, which, jnp.zeros((2 * half, HD), BF16))


def first_kernel(order_ref, q_ref, keys_ref, qt_ref, e_ref, acc_ref, stat_ref, s_ref):
    half = q_ref.shape[0] // 2
    heads = q_ref.shape[1] // HD
    cols = heads * half
    stretches, offsets = stretches_of(order_ref, half)
    for t in range(2):
        for h in range(heads):
            block = q_ref[pl.ds(offsets[t], half), h * HD : (h + 1) * HD]
            start = t * cols + h * half
            qt_ref[:, start : start + half] = flip(block).astype(BF16)
    parity = lax.axis_index("core")
    results = forward(keys_ref, parity, stretches, qt_ref, s_ref, e_ref, acc_ref)
    for t in range(2):
        for k in range(2):
            stat_ref[2 * t + k] = results[t][k]


def second_kernel(
    order_ref,
    g_ref,
    keys_ref,
    qt_ref,
    old_acc_ref,
    old_stat_ref,
    out_ref,
    gt_ref,
    delta_ref,
    dkeys_ref,
    dq_acc_ref,
    s_ref,
    e_ref,
    acc_ref,
    own_gt_ref,
    own_delta_ref,
):
    half = g_ref.shape[0] // 2
    heads = g_ref.shape[1] // HD
    cols = heads * half
    stretches, offsets = stretches_of(order_ref, half)
    parity = 1 - lax.axis_index("core")
    results = forward(keys_ref, parity, stretches, qt_ref, s_ref, e_ref, acc_ref)
    for t in range(2):
        old_shift, old_total = old_stat_ref[2 * t], old_stat_ref[2 * t + 1]
        new_shift, new_total = results[t]
        shift = jnp.maximum(old_shift, new_shift)
        old_part = jnp.exp2(old_shift - shift)
        new_part = jnp.exp2(new_shift - shift)
        inverse = 1.0 / (old_total * old_part + new_total * new_part)
        old_part = old_part * inverse
        new_part = new_part * inverse
        for h in range(heads):
            part = slice(h * half, (h + 1) * half)
            full = slice(t * cols + h * half, t * cols + (h + 1) * half)
            column = slice(h * HD, (h + 1) * HD)
            total = old_acc_ref[t, :, part] * old_part[:, part]
            total = total + acc_ref[t, :, part] * new_part[:, part]
            out = total.astype(BF16)
            out_ref[pl.ds(offsets[t], half), column] = flip(out).astype(BF16)
            grad = flip(g_ref[pl.ds(offsets[t], half), column])
            gt_ref[:, full] = (grad * old_part[:, part]).astype(BF16)
            own_gt_ref[:, full] = (grad * new_part[:, part]).astype(BF16)
            delta = jnp.sum(grad * out.astype(F32), axis=0, keepdims=True)
            delta_ref[t, :, part] = delta * old_part[:, part]
            own_delta_ref[t, :, part] = delta * new_part[:, part]
        dq_acc_ref[t] = jnp.zeros(dq_acc_ref.shape[1:], F32)
    backward(
        keys_ref,
        parity,
        stretches,
        qt_ref,
        own_gt_ref,
        own_delta_ref,
        e_ref,
        dq_acc_ref,
        dkeys_ref,
    )


def third_kernel(
    order_ref,
    keys_ref,
    qt_ref,
    gt_ref,
    delta_ref,
    e_ref,
    old_acc_ref,
    dkeys_ref,
    dq_ref,
    acc_ref,
):
    half = dq_ref.shape[0] // 2
    heads = dq_ref.shape[1] // HD
    stretches, offsets = stretches_of(order_ref, half)
    parity = lax.axis_index("core")
    acc_ref[...] = old_acc_ref[...]
    backward(
        keys_ref,
        parity,
        stretches,
        qt_ref,
        gt_ref,
        delta_ref,
        e_ref,
        acc_ref,
        dkeys_ref,
    )
    for t in range(2):
        for h in range(heads):
            value = (acc_ref[t, :, h * half : (h + 1) * half] * SCALE).T.astype(BF16)
            dq_ref[pl.ds(offsets[t], half), h * HD : (h + 1) * HD] = value


def call(kernel, name, outs, scratch, flops, *args):
    vmem = pl.BlockSpec(memory_space=pltpu.VMEM)
    return pl.pallas_call(
        kernel,
        out_shape=tuple(jax.ShapeDtypeStruct(*out) for out in outs),
        in_specs=[pl.BlockSpec(memory_space=pltpu.SMEM)] + [vmem] * (len(args) - 1),
        out_specs=(vmem,) * len(outs),
        scratch_shapes=[pltpu.VMEM(*item) for item in scratch],
        compiler_params=pltpu.CompilerParams(vmem_limit_bytes=VMEM_BYTES),
        cost_estimate=pl.CostEstimate(
            flops=flops, bytes_accessed=8 << 20, transcendentals=0
        ),
        name=name,
    )(*args)


def shapes_of(queries, keys):
    rows, width = queries.shape
    half = rows // 2
    cols = width // HD * half
    slots = keys.shape[1] // 2 + keys.shape[1] // 4
    weights = (slots, 2 * half, cols)
    return dict(
        weights=(weights, BF16),
        scores=(weights, F32),
        flat=((HD, 2 * cols), BF16),
        acc=((2, HD, cols), F32),
        row=((2, 1, cols), F32),
        stat=((4, 1, cols), F32),
        keys=(keys.shape, BF16),
        queries=(queries.shape, BF16),
    )


def attend_mine(order, queries, mine):
    s = shapes_of(queries, mine)
    outs = (s["flat"], s["weights"], s["acc"], s["stat"])
    return call(
        first_kernel, "first", outs, (s["scores"],), 3 << 30, order, queries, mine
    )


def attend_theirs(order, grads, theirs, qt, acc, stat):
    s = shapes_of(grads, theirs)
    outs = (s["queries"], s["flat"], s["row"], s["keys"], s["acc"])
    scratch = (s["scores"], s["weights"], s["acc"], s["flat"], s["row"])
    return call(
        second_kernel, "second", outs, scratch, 6 << 30, order, grads, theirs, qt, acc, stat
    )


def finish_mine(order, queries, mine, qt, gt, delta, weights, acc):
    s = shapes_of(queries, mine)
    outs = (s["keys"], s["queries"])
    return call(
        third_kernel,
        "third",
        outs,
        (s["acc"],),
        4 << 30,
        order,
        mine,
        qt,
        gt,
        delta,
        weights,
        acc,
    )


AXES = ("zl", "xh", "xl", "core", "y", "zh")
SPREAD = ("zl", "xh", "xl", "zh")
SWAP = ((0, 1), (1, 0))


def per_device(queries, key_vectors, value_vectors, out_grads, pair_order):
    sizes = {name: lax.axis_size(name) for name in AXES}
    zl, xh, xl, zh = (sizes[name] for name in SPREAD)
    rows = key_vectors.shape[0]
    kv_heads = key_vectors.shape[1] // HD
    runs = sizes["y"]
    pairs = zl * xh * xl

    both = jnp.stack([key_vectors, value_vectors]).reshape(2, rows, kv_heads, HD)
    sent = both.transpose(2, 0, 1, 3).reshape(zl, xh, 1, 1, 2, rows, HD)
    sent = jnp.broadcast_to(sent, (zl, xh, xl, zh, 2, rows, HD))
    sent = sent.reshape(pairs * zh, 2, rows, HD)
    got = lax.all_to_all(sent, SPREAD, split_axis=0, concat_axis=0, tiled=True)
    run = got.reshape(pairs, zh, 2, rows, HD).transpose(0, 2, 1, 3, 4)
    run = run.reshape(1, pairs, 2, zh * rows, HD)
    whole = jnp.broadcast_to(run, (runs,) + run.shape[1:])
    mine = lax.all_to_all(whole, "y", split_axis=0, concat_axis=0, tiled=True)
    theirs = lax.ppermute(mine, "core", SWAP)

    qt, weights, acc, stat = attend_mine(pair_order, queries, mine)
    attended, gt, delta, dtheirs, acc = attend_theirs(
        pair_order, out_grads, theirs, qt, acc, stat
    )
    other = lax.ppermute(dtheirs, "core", SWAP)
    dmine, query_grads = finish_mine(
        pair_order, queries, mine, qt, gt, delta, weights, acc
    )
    total = (dmine.astype(F32) + other.astype(F32)).astype(BF16)
    got = lax.all_to_all(total, "y", split_axis=0, concat_axis=0, tiled=True)
    total = got.astype(F32).sum(axis=0).astype(BF16)
    total = total.reshape(pairs, 2, zh, rows, HD).transpose(0, 2, 1, 3, 4)
    total = total.reshape(pairs * zh, 2, rows, HD)
    got = lax.all_to_all(total, SPREAD, split_axis=0, concat_axis=0, tiled=True)
    total = got.reshape(kv_heads, xl * zh, 2, rows, HD).astype(F32).sum(axis=1)
    total = total.transpose(1, 2, 0, 3).reshape(2, rows, kv_heads * HD)
    return attended, query_grads, total[0], total[1]


def solution(mesh):
    fine = Mesh(mesh.devices.reshape(4, 2, 2, 2, 8, 2), AXES)
    fsdp, cp = AXES[:4], AXES[4:]
    return jax.shard_map(
        per_device,
        mesh=fine,
        in_specs=(P(cp, fsdp), P(AXES, None), P(AXES, None), P(cp, fsdp), P()),
        out_specs=(P(cp, fsdp), P(cp, fsdp), P(AXES, None), P(AXES, None)),
        check_vma=False,
    )
```

time: 132 us -> 133 us (level); the launches traced: 132 us -> 131 us
  Pallas kernels: 16.9 us -> 22 us
  waiting for transfers between devices: 4.53 us -> 0.01 us
  blocking collectives: 99.4 us -> 97.9 us
    pallas_call x1 -> x3, Pallas kernels: 16.9 us -> 22 us  [call(): pl.pallas_call(kernel, out_shape=tuple((jax.ShapeDtypeStruct(*out) for ou...]
    ppermute x1, waiting for transfers between devices: 2.26 us -> 0.01 us  [per_device(): theirs = lax.ppermute(mine, 'core', SWAP)]
    ppermute x1, waiting for transfers between devices: 2.26 us -> 0.01 us  [per_device(): other = lax.ppermute(dtheirs, 'core', SWAP)]
    all_to_all x1, blocking collectives: 31.6 us -> 30.2 us  [per_device(): got = lax.all_to_all(total, 'y', split_axis=0, concat_axis=0, tiled=True)]
  transfers between devices with their start and end apart: 2 -> 2, of which waited for: 2 -> 0; matrix products, arithmetic and copies ran while one was open for 0% -> 0% of each run, Pallas kernels for 0% -> 9%
where the time goes in v2:
time: 133 us; the launch traced here: 131 us
  blocking collectives  97.9 us (74%)
  Pallas kernels  22 us (17%)
  starting transfers between devices  7.81 us (6%)
    all_to_all x1, blocking collectives, per_device(): mine = lax.all_to_all(whole, 'y', split_axis=0, concat_axis=0, tiled=True)  32.4 us
    all_to_all x1, blocking collectives, per_device(): got = lax.all_to_all(total, 'y', split_axis=0, concat_axis=0, tiled=True)  30.2 us
    all_to_all x1, blocking collectives, per_device(): got = lax.all_to_all(sent, SPREAD, split_axis=0, concat_axis=0, tiled=True)  22.6 us
    pallas_call x3, Pallas kernels, call(): pl.pallas_call(kernel, out_shape=tuple((jax.ShapeDtypeStruct(*out) for ou...  22 us
    all_to_all x1, blocking collectives, per_device(): got = lax.all_to_all(total, SPREAD, split_axis=0, concat_axis=0, tiled=True)  12.6 us
    ppermute x1, starting transfers between devices, per_device(): theirs = lax.ppermute(mine, 'core', SWAP)  5.9 us
  transfers between devices with their start and end apart: 2, of which 0 were waited for; matrix products, arithmetic and copies ran while one was open for 0% of the time, Pallas kernels for 9%

profile of v2, /device:TPU:1, one launch (start us, length us, event | category | flops | bytes accessed | tf_op | source)
XLA Modules:
  0.0 130.6 jit_solution(8900223351565178657)
XLA Ops:
  0.6 0.0 copy-start.2
  0.6 0.0 copy-start
  0.7 0.8 pad_maximum_fusion.1
  1.5 22.6 %all_to_all.20 = bf16[32,2,8,128]{3,2,1,0:T(8,128)(2,1)S(1)} all-to-all(bf16[32,2,8,128]{3,2,1,0:T(8,128)(2,1)S(1)} %bitcast.22), channel_id=1, replica_groups=mesh['zl'=4,'xh'=2,'xl'=2,'core'=2,'y'=8,'zh'=2] {'zl','xh','xl','zh'}, dimensions={0} | all-to-all | bytes 262144 | tf_op jit(solution)/shard_map/all_to_all | solution.py:342
  24.1 0.2 broadcast_in_dim.17
  24.3 32.4 %all_to_all.21.keys_ref = bf16[8,16,2,16,128]{4,3,2,1,0:T(8,128)(2,1)S(1)} all-to-all(bf16[8,16,2,16,128]{4,3,2,1,0:T(8,128)(2,1)S(1)} %broadcast_in_dim.17), channel_id=1, replica_groups=mesh['zl'=4,'xh'=2,'xl'=2,'core'=2,'y'=8,'zh'=2] {'y'}, dimensions={0} | all-to-all | bytes 2097152 | tf_op jit(solution)/shard_map/all_to_all | solution.py:346
  56.7 0.0 copy-start.1
  56.7 5.9 %collective-permute-start = (bf16[8,16,2,16,128]{4,3,2,1,0:T(8,128)(2,1)S(1)}, bf16[8,16,2,16,128]{4,3,2,1,0:T(8,128)(2,1)S(1)}, u32[]{:S(2)}, u32[]{:S(2)}) collective-permute-start(bf16[8,16,2,16,128]{4,3,2,1,0:T(8,128)(2,1)S(1)} %all_to_all.21.keys_ref), channel_id=1, source_target_pairs={{0,16},{16,0},{1,17},{17,1},{2,18},{18,2},{3,19},{19,3},{4,20},{20... | collective-permute-start | bytes 3145736 | tf_op jit(solution)/shard_map/ppermute | solution.py:347
  62.7 0.0 copy-done.2
  62.7 0.0 copy-done
  62.7 5.2 %first.1 = (bf16[128,1024]{1,0:T(8,128)(2,1)S(1)}, bf16[12,256,512]{2,1,0:T(8,128)(2,1)S(1)}, f32[2,128,512]{2,1,0:T(8,128)S(1)}, f32[4,1,512]{2,1,0:T(1,128)S(1)}) custom-call(s32[32]{0:T(128)S(1)} %copy-done.2, bf16[256,512]{1,0:T(8,128)(2,1)S(1)} %copy-done, bf16[8,16,2,16,128]{4,3,2,1,0:T(8,128)(2,1)S(1)} %all_to_all.21.keys_ref), custom_call_target="tpu_custom_call" | custom-call | flops 3221225472 | bytes 8388608 | tf_op jit(solution)/shard_map/first/pallas_call | solution.py:257
  67.9 0.0 collective-permute-done.keys_ref
  67.9 0.0 copy-done.1
  67.9 10.6 %second.1 = (bf16[256,512]{1,0:T(8,128)(2,1)}, bf16[128,1024]{1,0:T(8,128)(2,1)S(1)}, f32[2,1,512]{2,1,0:T(1,128)S(1)}, bf16[8,16,2,16,128]{4,3,2,1,0:T(8,128)(2,1)S(1)}, f32[2,128,512]{2,1,0:T(8,128)S(1)}) custom-call(s32[32]{0:T(128)S(1)} %copy-done.2, bf16[256,512]{1,0:T(8,128)(2,1)S(1)} %copy-done.1, ...), custom_call_target="tpu_custom_call" | custom-call | flops 6442450944 | bytes 8388608 | tf_op jit(solution)/shard_map/second/pallas_call | solution.py:257
  78.5 1.9 %collective-permute-start.1 = (bf16[8,16,2,16,128]{4,3,2,1,0:T(8,128)(2,1)S(1)}, bf16[8,16,2,16,128]{4,3,2,1,0:T(8,128)(2,1)S(1)}, u32[]{:S(2)}, u32[]{:S(2)}) collective-permute-start(bf16[8,16,2,16,128]{4,3,2,1,0:T(8,128)(2,1)S(1)} %get-tuple-element.25), channel_id=1, source_target_pairs={{0,16},{16,0},{1,17},{17,1},{2,18},{18,2},{3,19},{19,3},{4,20},{20... | collective-permute-start | bytes 3145736 | tf_op jit(solution)/shard_map/ppermute | solution.py:353
  80.4 6.2 %third.1 = (bf16[8,16,2,16,128]{4,3,2,1,0:T(8,128)(2,1)S(1)}, bf16[256,512]{1,0:T(8,128)(2,1)}) custom-call(s32[32]{0:T(128)S(1)} %copy-done.2, bf16[8,16,2,16,128]{4,3,2,1,0:T(8,128)(2,1)S(1)} %all_to_all.21.keys_ref, bf16[128,1024]{1,0:T(8,128)(2,1)S(1)} %get-tuple-element.15.qt_ref, bf16[128,1024]{1,0:T(8,128)(2,1)S(1)} %get-tuple-element.19.gt_ref, ...), custom_call_target="tpu_custom_call" | custom-call | flops 4294967296 | bytes 8388608 | tf_op jit(solution)/shard_map/third/pallas_call | solution.py:257
  86.6 0.0 collective-permute-done.1
  86.6 0.3 add_convert_fusion
  86.9 30.2 %all_to_all.22 = bf16[8,16,2,16,128]{4,3,2,1,0:T(8,128)(2,1)S(1)} all-to-all(bf16[8,16,2,16,128]{4,3,2,1,0:T(8,128)(2,1)S(1)} %add_convert_fusion), channel_id=1, replica_groups=mesh['zl'=4,'xh'=2,'xl'=2,'core'=2,'y'=8,'zh'=2] {'y'}, dimensions={0} | all-to-all | bytes 2097152 | tf_op jit(solution)/shard_map/all_to_all | solution.py:358
  117.1 0.1 reduce_sum.21
  117.3 12.6 %all_to_all.23 = bf16[32,2,8,128]{3,2,1,0:T(8,128)(2,1)S(1)} all-to-all(bf16[32,2,8,128]{3,2,1,0:T(8,128)(2,1)S(1)} %bitcast.23), channel_id=1, replica_groups=mesh['zl'=4,'xh'=2,'xl'=2,'core'=2,'y'=8,'zh'=2] {'zl','xh','xl','zh'}, dimensions={0} | all-to-all | bytes 262144 | tf_op jit(solution)/shard_map/all_to_all | solution.py:362
  130.0 0.6 slice_bitcast_fusion
  (6 shorter events, 0.1 us)
Async XLA Ops:
  0.6 62.0 %copy-start.2 = (s32[32]{0:T(128)S(1)}, s32[32]{0:T(128)}, u32[]{:S(2)}) copy-start(s32[32]{0:T(128)} %order_ref.5) | copy-start | bytes 388
  0.6 62.0 %copy-start = (bf16[256,512]{1,0:T(8,128)(2,1)S(1)}, bf16[256,512]{1,0:T(8,128)(2,1)}, u32[]{:S(2)}) copy-start(bf16[256,512]{1,0:T(8,128)(2,1)} %q_ref.1) | copy-start | bytes 786436
  56.7 11.1 %copy-start.1 = (bf16[256,512]{1,0:T(8,128)(2,1)S(1)}, bf16[256,512]{1,0:T(8,128)(2,1)}, u32[]{:S(2)}) copy-start(bf16[256,512]{1,0:T(8,128)(2,1)} %g_ref.1) | copy-start | bytes 786436
  56.7 11.1 %collective-permute-start = (bf16[8,16,2,16,128]{4,3,2,1,0:T(8,128)(2,1)S(1)}, bf16[8,16,2,16,128]{4,3,2,1,0:T(8,128)(2,1)S(1)}, u32[]{:S(2)}, u32[]{:S(2)}) collective-permute-start(bf16[8,16,2,16,128]{4,3,2,1,0:T(8,128)(2,1)S(1)} %all_to_all.21.keys_ref), channel_id=1, source_target_pairs={{0,16},{16,0},{1,17},{17,1},{2,18},{18,2},{3,19},{19,3},{4,20},{20... | collective-permute-start | bytes 3145736 | tf_op jit(solution)/shard_map/ppermute | solution.py:347
  78.5 8.1 %collective-permute-start.1 = (bf16[8,16,2,16,128]{4,3,2,1,0:T(8,128)(2,1)S(1)}, bf16[8,16,2,16,128]{4,3,2,1,0:T(8,128)(2,1)S(1)}, u32[]{:S(2)}, u32[]{:S(2)}) collective-permute-start(bf16[8,16,2,16,128]{4,3,2,1,0:T(8,128)(2,1)S(1)} %get-tuple-element.25), channel_id=1, source_target_pairs={{0,16},{16,0},{1,17},{17,1},{2,18},{18,2},{3,19},{19,3},{4,20},{20... | collective-permute-start | bytes 3145736 | tf_op jit(solution)/shard_map/ppermute | solution.py:353

commit v3 on v2

--- a/solution.py
+++ b/solution.py
@@ -13,6 +13,8 @@
 RATE = SCALE * math.log2(math.e)
 FILL = -1e30
 VMEM_BYTES = 32 << 20
+CHUNK = 64
+GROUP = 4
 
 
 def dot(a, b, a_axis, b_axis):
@@ -42,31 +44,44 @@
 
 
 def block_of(ref, index, which):
-    runs, _, _, grain, _ = ref.shape
-    parts = [ref[:, 2 * index + u, which].reshape(runs * grain, HD) for u in range(2)]
-    return jnp.concatenate(parts, axis=0)
+    runs, _, slices, _, grain, _ = ref.shape
+    parts = [
+        ref[:, 2 * index + u, :, which].astype(F32).reshape(runs * slices * grain, HD)
+        for u in range(2)
+    ]
+    return jnp.concatenate(parts, axis=0).astype(BF16)
+
+
+def wide(ref, first, count):
+    return jnp.concatenate([ref[first + k] for k in range(count)], axis=1)
 
 
 def forward(keys_ref, parity, stretches, qt_ref, s_ref, e_ref, acc_ref):
-    cols = s_ref.shape[2]
+    rows, cols = s_ref.shape[1:]
     blocks = keys_ref.shape[1] // 2
-    half = s_ref.shape[1] // 2
+    half = rows // 2
+    heads = cols // half
     counts = counts_of(stretches, parity)
     bases = (0, blocks)
     shifts = []
     for t in range(2):
-        span = slice(t * cols, (t + 1) * cols)
 
         def score(index, peak, masked):
-            s = dot(block_of(keys_ref, index, 0), qt_ref[:, span], 1, 0)
-            if masked:
-                j = lax.broadcasted_iota(jnp.int32, s.shape, 0)
-                r = lax.rem(lax.broadcasted_iota(jnp.int32, s.shape, 1), half)
-                j = j + jnp.where(j >= half, half, 0)
-                ahead = (4 * index + parity - stretches[t]) * half
-                s = jnp.where(j + ahead <= r, s, FILL)
-            s_ref[bases[t] + index] = s
-            return jnp.maximum(peak, jnp.max(s.reshape(-1, 8, cols), axis=0))
+            keys = block_of(keys_ref, index, 0)
+            peaks = []
+            for c in range(0, heads, GROUP):
+                span = slice(c * half, (c + GROUP) * half)
+                s = dot(keys, wide(qt_ref, t * heads + c, GROUP), 1, 0)
+                if masked:
+                    j = lax.broadcasted_iota(jnp.int32, s.shape, 0)
+                    r = lax.rem(lax.broadcasted_iota(jnp.int32, s.shape, 1), half)
+                    j = j + jnp.where(j >= half, half, 0)
+                    ahead = (4 * index + parity - stretches[t]) * half
+                    s = jnp.where(j + ahead <= r, s, FILL)
+                s_ref[bases[t] + index, :, span] = s
+                high = jnp.max(s.reshape(-1, 8, GROUP * half), axis=0)
+                peaks.append(jnp.maximum(peak[:, span], high))
+            return jnp.concatenate(peaks, axis=1)
 
         last = counts[t] - 1
         peak = jnp.full((8, cols), FILL, F32)
@@ -78,53 +93,68 @@
     for t in range(2):
 
         def weigh(index, total):
-            e = jnp.exp2(s_ref[bases[t] + index] * RATE - shifts[t])
-            e_ref[bases[t] + index] = e.astype(BF16)
-            return total + jnp.sum(e.reshape(-1, 8, cols), axis=0)
+            slot = bases[t] + index
+            totals = []
+            for h in range(heads):
+                span = slice(h * half, (h + 1) * half)
+                shift = shifts[t][:, span]
+                part = total[:, span]
+                for start in range(0, rows, CHUNK):
+                    chunk = slice(start, start + CHUNK)
+                    e = jnp.exp2(s_ref[slot, chunk, span] * RATE - shift)
+                    e_ref[slot, h, chunk] = e.astype(BF16)
+                    part = part + jnp.sum(e.reshape(-1, 8, half), axis=0)
+                totals.append(part)
+            return jnp.concatenate(totals, axis=1)
 
         def attend(index):
-            return dot(block_of(keys_ref, index, 1), e_ref[bases[t] + index], 0, 0)
+            values = block_of(keys_ref, index, 1)
+            for c in range(0, heads, GROUP):
+                span = slice(c * half, (c + GROUP) * half)
+                weights = wide(e_ref.at[bases[t] + index], c, GROUP)
+                acc_ref[t, :, span] += dot(values, weights, 0, 0)
 
         def step(index, total):
-            acc_ref[t] += attend(index - 1)
+            attend(index - 1)
             return weigh(index, total)
 
         acc_ref[t] = jnp.zeros(acc_ref.shape[1:], F32)
         total = weigh(0, jnp.zeros((8, cols), F32))
         total = lax.fori_loop(1, counts[t], step, total)
-        acc_ref[t] += attend(counts[t] - 1)
+        attend(counts[t] - 1)
         results.append((shifts[t], jnp.sum(total, axis=0, keepdims=True)))
     return results
 
 
 def backward(keys_ref, parity, stretches, qt_ref, gt_ref, delta_ref, e_ref, acc_ref, out_ref):
-    runs, pairs, _, grain, _ = keys_ref.shape
-    cols = qt_ref.shape[1] // 2
-    half = runs * grain
+    runs, pairs, slices, _, grain, _ = keys_ref.shape
+    heads = qt_ref.shape[0] // 2
+    half = runs * slices * grain
     blocks = pairs // 2
     counts = counts_of(stretches, parity)
 
     def store(index, which, value):
         for u in range(2):
-            part = value[u * half : (u + 1) * half].reshape(runs, grain, HD)
-            out_ref[:, 2 * index + u, which] = part
+            part = value[u * half : (u + 1) * half].reshape(runs, slices, grain, HD)
+            out_ref[:, 2 * index + u, :, which] = part.astype(BF16)
 
     def pull(index, both):
         keys = block_of(keys_ref, index, 0)
         values = block_of(keys_ref, index, 1)
-        key_term = value_term = None
+        key_term = value_term = 0.0
         for t in range(2 if both else 1):
-            span = slice(t * cols, (t + 1) * cols)
-            weight = e_ref[index if t == 0 else blocks + index]
-            slope = dot(values, gt_ref[:, span], 1, 0) - delta_ref[t]
-            ds = (weight.astype(F32) * slope).astype(BF16)
-            acc_ref[t] += dot(keys, ds, 0, 0)
-            value_part = dot(gt_ref[:, span], weight, 1, 1)
-            key_part = dot(qt_ref[:, span], ds, 1, 1)
-            value_term = value_part if t == 0 else value_term + value_part
-            key_term = key_part if t == 0 else key_term + key_part
-        store(index, 0, (key_term * SCALE).T.astype(BF16))
-        store(index, 1, value_term.T.astype(BF16))
+            slot = index if t == 0 else blocks + index
+            for c in range(0, heads, GROUP):
+                span = slice(c * half, (c + GROUP) * half)
+                weights = wide(e_ref.at[slot], c, GROUP)
+                grads = wide(gt_ref, t * heads + c, GROUP)
+                slope = dot(values, grads, 1, 0) - delta_ref[t, :, span]
+                ds = (weights.astype(F32) * slope).astype(BF16)
+                value_term = value_term + dot(grads, weights, 1, 1)
+                key_term = key_term + dot(wide(qt_ref, t * heads + c, GROUP), ds, 1, 1)
+                acc_ref[t, :, span] += dot(keys, ds, 0, 0)
+        store(index, 0, (key_term * SCALE).T)
+        store(index, 1, value_term.T)
 
     @pl.loop(0, counts[1])
     def _(index):
@@ -137,19 +167,17 @@
     @pl.loop(counts[0], blocks)
     def _(index):
         for which in range(2):
-            store(index, which, jnp.zeros((2 * half, HD), BF16))
+            store(index, which, jnp.zeros((2 * half, HD), F32))
 
 
 def first_kernel(order_ref, q_ref, keys_ref, qt_ref, e_ref, acc_ref, stat_ref, s_ref):
     half = q_ref.shape[0] // 2
     heads = q_ref.shape[1] // HD
-    cols = heads * half
     stretches, offsets = stretches_of(order_ref, half)
     for t in range(2):
         for h in range(heads):
             block = q_ref[pl.ds(offsets[t], half), h * HD : (h + 1) * HD]
-            start = t * cols + h * half
-            qt_ref[:, start : start + half] = flip(block).astype(BF16)
+            qt_ref[t * heads + h] = flip(block).astype(BF16)
     parity = lax.axis_index("core")
     results = forward(keys_ref, parity, stretches, qt_ref, s_ref, e_ref, acc_ref)
     for t in range(2):
@@ -177,7 +205,6 @@
 ):
     half = g_ref.shape[0] // 2
     heads = g_ref.shape[1] // HD
-    cols = heads * half
     stretches, offsets = stretches_of(order_ref, half)
     parity = 1 - lax.axis_index("core")
     results = forward(keys_ref, parity, stretches, qt_ref, s_ref, e_ref, acc_ref)
@@ -192,15 +219,14 @@
         new_part = new_part * inverse
         for h in range(heads):
             part = slice(h * half, (h + 1) * half)
-            full = slice(t * cols + h * half, t * cols + (h + 1) * half)
             column = slice(h * HD, (h + 1) * HD)
             total = old_acc_ref[t, :, part] * old_part[:, part]
             total = total + acc_ref[t, :, part] * new_part[:, part]
             out = total.astype(BF16)
             out_ref[pl.ds(offsets[t], half), column] = flip(out).astype(BF16)
             grad = flip(g_ref[pl.ds(offsets[t], half), column])
-            gt_ref[:, full] = (grad * old_part[:, part]).astype(BF16)
-            own_gt_ref[:, full] = (grad * new_part[:, part]).astype(BF16)
+            gt_ref[t * heads + h] = (grad * old_part[:, part]).astype(BF16)
+            own_gt_ref[t * heads + h] = (grad * new_part[:, part]).astype(BF16)
             delta = jnp.sum(grad * out.astype(F32), axis=0, keepdims=True)
             delta_ref[t, :, part] = delta * old_part[:, part]
             own_delta_ref[t, :, part] = delta * new_part[:, part]
@@ -273,11 +299,11 @@
     half = rows // 2
     cols = width // HD * half
     slots = keys.shape[1] // 2 + keys.shape[1] // 4
-    weights = (slots, 2 * half, cols)
+    heads = cols // half
     return dict(
-        weights=(weights, BF16),
-        scores=(weights, F32),
-        flat=((HD, 2 * cols), BF16),
+        weights=((slots, heads, 2 * half, half), BF16),
+        scores=((slots, 2 * half, cols), F32),
+        flat=((2 * heads, HD, half), BF16),
         acc=((2, HD, cols), F32),
         row=((2, 1, cols), F32),
         stat=((4, 1, cols), F32),
@@ -323,27 +349,24 @@
 
 
 AXES = ("zl", "xh", "xl", "core", "y", "zh")
-SPREAD = ("zl", "xh", "xl", "zh")
+SPREAD = ("y", "zl", "xh", "xl", "zh")
 SWAP = ((0, 1), (1, 0))
 
 
 def per_device(queries, key_vectors, value_vectors, out_grads, pair_order):
     sizes = {name: lax.axis_size(name) for name in AXES}
-    zl, xh, xl, zh = (sizes[name] for name in SPREAD)
+    runs, zl, xh, xl, zh = (sizes[name] for name in SPREAD)
     rows = key_vectors.shape[0]
     kv_heads = key_vectors.shape[1] // HD
-    runs = sizes["y"]
     pairs = zl * xh * xl
+    block = (2, rows, HD)
 
     both = jnp.stack([key_vectors, value_vectors]).reshape(2, rows, kv_heads, HD)
-    sent = both.transpose(2, 0, 1, 3).reshape(zl, xh, 1, 1, 2, rows, HD)
-    sent = jnp.broadcast_to(sent, (zl, xh, xl, zh, 2, rows, HD))
-    sent = sent.reshape(pairs * zh, 2, rows, HD)
-    got = lax.all_to_all(sent, SPREAD, split_axis=0, concat_axis=0, tiled=True)
-    run = got.reshape(pairs, zh, 2, rows, HD).transpose(0, 2, 1, 3, 4)
-    run = run.reshape(1, pairs, 2, zh * rows, HD)
-    whole = jnp.broadcast_to(run, (runs,) + run.shape[1:])
-    mine = lax.all_to_all(whole, "y", split_axis=0, concat_axis=0, tiled=True)
+    sent = both.transpose(2, 0, 1, 3).reshape((1, zl, xh, 1, 1) + block)
+    sent = jnp.broadcast_to(sent, (runs, zl, xh, xl, zh) + block)
+    sent = sent.reshape((runs * pairs * zh,) + block)
+    mine = lax.all_to_all(sent, SPREAD, split_axis=0, concat_axis=0, tiled=True)
+    mine = mine.reshape((runs, pairs, zh) + block)
     theirs = lax.ppermute(mine, "core", SWAP)
 
     qt, weights, acc, stat = attend_mine(pair_order, queries, mine)
@@ -355,12 +378,10 @@
         pair_order, queries, mine, qt, gt, delta, weights, acc
     )
     total = (dmine.astype(F32) + other.astype(F32)).astype(BF16)
-    got = lax.all_to_all(total, "y", split_axis=0, concat_axis=0, tiled=True)
-    total = got.astype(F32).sum(axis=0).astype(BF16)
-    total = total.reshape(pairs, 2, zh, rows, HD).transpose(0, 2, 1, 3, 4)
-    total = total.reshape(pairs * zh, 2, rows, HD)
+    total = total.reshape((runs * pairs * zh,) + block)
     got = lax.all_to_all(total, SPREAD, split_axis=0, concat_axis=0, tiled=True)
-    total = got.reshape(kv_heads, xl * zh, 2, rows, HD).astype(F32).sum(axis=1)
+    got = got.reshape((runs, kv_heads, xl * zh) + block)
+    total = got.astype(F32).sum(axis=(0, 2))
     total = total.transpose(1, 2, 0, 3).reshape(2, rows, kv_heads * HD)
     return attended, query_grads, total[0], total[1]
 

time: 133 us -> 123 us (0.925)
  blocking collectives: 97.9 us -> 89.8 us
    all_to_all x3 -> x1, blocking collectives: 85.3 us -> 51.5 us  [per_device(): mine = lax.all_to_all(sent, SPREAD, split_axis=0, concat_axis=0, tiled=True)]
    all_to_all x1, blocking collectives: 12.6 us -> 38.2 us  [per_device(): got = lax.all_to_all(total, SPREAD, split_axis=0, concat_axis=0, tiled=True)]
where the time goes in v3:
time: 123 us; the launch traced here: 121 us
  blocking collectives  89.8 us (73%)
  Pallas kernels  21.1 us (17%)
  starting transfers between devices  7.02 us (6%)
    all_to_all x1, blocking collectives, per_device(): mine = lax.all_to_all(sent, SPREAD, split_axis=0, concat_axis=0, tiled=True)  51.5 us
    all_to_all x1, blocking collectives, per_device(): got = lax.all_to_all(total, SPREAD, split_axis=0, concat_axis=0, tiled=True)  38.2 us
    pallas_call x3, Pallas kernels, call(): pl.pallas_call(kernel, out_shape=tuple((jax.ShapeDtypeStruct(*out) for ou...  21.1 us
    ppermute x1, starting transfers between devices, per_device(): theirs = lax.ppermute(mine, 'core', SWAP)  5.1 us
  transfers between devices with their start and end apart: 2, of which 0 were waited for; matrix products, arithmetic and copies ran while one was open for 0% of the time, Pallas kernels for 9%

profile of v3, /device:TPU:1, one launch (start us, length us, event | category | flops | bytes accessed | tf_op | source)
XLA Modules:
  0.0 120.7 jit_solution(18116791749396652829)
XLA Ops:
  0.6 0.0 copy-start.2
  0.6 0.0 copy-start
  0.7 0.8 pad_maximum_fusion
  1.4 0.2 broadcast_in_dim.8
  1.7 51.5 %all_to_all.10 = bf16[256,2,8,128]{3,2,1,0:T(8,128)(2,1)S(1)} all-to-all(bf16[256,2,8,128]{3,2,1,0:T(8,128)(2,1)S(1)} %bitcast.19), channel_id=1, replica_groups=mesh['zl'=4,'xh'=2,'xl'=2,'core'=2,'y'=8,'zh'=2] {'y','zl','xh','xl','zh'}, dimensions={0} | all-to-all | bytes 2097152 | tf_op jit(solution)/shard_map/all_to_all | solution.py:368
  53.2 0.0 copy-start.1
  53.2 5.1 %collective-permute-start = (bf16[8,16,2,2,8,128]{5,4,3,2,1,0:T(8,128)(2,1)S(1)}, bf16[8,16,2,2,8,128]{5,4,3,2,1,0:T(8,128)(2,1)S(1)}, u32[]{:S(2)}, u32[]{:S(2)}) collective-permute-start(bf16[8,16,2,2,8,128]{5,4,3,2,1,0:T(8,128)(2,1)S(1)} %bitcast.15), channel_id=1, source_target_pairs={{0,16},{16,0},{1,17},{17,1},{2,18},{18,2},{3,19},{19,3},{4,20},{20... | collective-permute-start | bytes 3145736 | tf_op jit(solution)/shard_map/ppermute | solution.py:370
  58.3 0.0 copy-done.2
  58.3 0.0 copy-done
  58.3 5.1 %first.1 = (bf16[8,128,128]{2,1,0:T(8,128)(2,1)S(1)}, bf16[12,4,256,128]{3,2,1,0:T(8,128)(2,1)S(1)}, f32[2,128,512]{2,1,0:T(8,128)S(1)}, f32[4,1,512]{2,1,0:T(1,128)S(1)}) custom-call(s32[32]{0:T(128)S(1)} %copy-done.2, bf16[256,512]{1,0:T(8,128)(2,1)S(1)} %copy-done, bf16[8,16,2,2,8,128]{5,4,3,2,1,0:T(8,128)(2,1)S(1)} %bitcast.16), custom_call_target="tpu_custom_call" | custom-call | flops 3221225472 | bytes 8388608 | tf_op jit(solution)/shard_map/first/pallas_call | solution.py:283
  63.5 0.0 collective-permute-done.keys_ref
  63.5 0.0 copy-done.1
  63.5 10.2 %second.1 = (bf16[256,512]{1,0:T(8,128)(2,1)}, bf16[8,128,128]{2,1,0:T(8,128)(2,1)S(1)}, f32[2,1,512]{2,1,0:T(1,128)S(1)}, bf16[8,16,2,2,8,128]{5,4,3,2,1,0:T(8,128)(2,1)S(1)}, f32[2,128,512]{2,1,0:T(8,128)S(1)}) custom-call(s32[32]{0:T(128)S(1)} %copy-done.2, bf16[256,512]{1,0:T(8,128)(2,1)S(1)} %copy-done.1, ...), custom_call_target="tpu_custom_call" | custom-call | flops 6442450944 | bytes 8388608 | tf_op jit(solution)/shard_map/second/pallas_call | solution.py:283
  73.7 1.9 %collective-permute-start.1 = (bf16[8,16,2,2,8,128]{5,4,3,2,1,0:T(8,128)(2,1)S(1)}, bf16[8,16,2,2,8,128]{5,4,3,2,1,0:T(8,128)(2,1)S(1)}, u32[]{:S(2)}, u32[]{:S(2)}) collective-permute-start(bf16[8,16,2,2,8,128]{5,4,3,2,1,0:T(8,128)(2,1)S(1)} %get-tuple-element.25), channel_id=1, source_target_pairs={{0,16},{16,0},{1,17},{17,1},{2,18},{18,2},{3,19},{19,3},{4,20},{20... | collective-permute-start | bytes 3145736 | tf_op jit(solution)/shard_map/ppermute | solution.py:376
  75.6 5.7 %third.1 = (bf16[8,16,2,2,8,128]{5,4,3,2,1,0:T(8,128)(2,1)S(1)}, bf16[256,512]{1,0:T(8,128)(2,1)}) custom-call(s32[32]{0:T(128)S(1)} %copy-done.2, bf16[8,16,2,2,8,128]{5,4,3,2,1,0:T(8,128)(2,1)S(1)} %bitcast.17, bf16[8,128,128]{2,1,0:T(8,128)(2,1)S(1)} %get-tuple-element.15.qt_ref, bf16[8,128,128]{2,1,0:T(8,128)(2,1)S(1)} %get-tuple-element.19.gt_ref, ...), custom_call_target="tpu_custom_call" | custom-call | flops 4294967296 | bytes 8388608 | tf_op jit(solution)/shard_map/third/pallas_call | solution.py:283
  81.4 0.0 collective-permute-done.1
  81.4 0.3 add_convert_fusion
  81.6 38.2 %all_to_all.11 = bf16[256,2,8,128]{3,2,1,0:T(8,128)(2,1)S(1)} all-to-all(bf16[256,2,8,128]{3,2,1,0:T(8,128)(2,1)S(1)} %bitcast.18), channel_id=1, replica_groups=mesh['zl'=4,'xh'=2,'xl'=2,'core'=2,'y'=8,'zh'=2] {'y','zl','xh','xl','zh'}, dimensions={0} | all-to-all | bytes 2097152 | tf_op jit(solution)/shard_map/all_to_all | solution.py:382
  119.9 0.2 convert_reduce_fusion
  120.0 0.6 slice_bitcast_fusion
  (1 shorter events, 0.0 us)
Async XLA Ops:
  0.6 57.7 %copy-start.2 = (s32[32]{0:T(128)S(1)}, s32[32]{0:T(128)}, u32[]{:S(2)}) copy-start(s32[32]{0:T(128)} %order_ref.5) | copy-start | bytes 388
  0.6 57.7 %copy-start = (bf16[256,512]{1,0:T(8,128)(2,1)S(1)}, bf16[256,512]{1,0:T(8,128)(2,1)}, u32[]{:S(2)}) copy-start(bf16[256,512]{1,0:T(8,128)(2,1)} %q_ref.1) | copy-start | bytes 786436
  53.2 10.3 %copy-start.1 = (bf16[256,512]{1,0:T(8,128)(2,1)S(1)}, bf16[256,512]{1,0:T(8,128)(2,1)}, u32[]{:S(2)}) copy-start(bf16[256,512]{1,0:T(8,128)(2,1)} %g_ref.1) | copy-start | bytes 786436
  53.2 10.3 %collective-permute-start = (bf16[8,16,2,2,8,128]{5,4,3,2,1,0:T(8,128)(2,1)S(1)}, bf16[8,16,2,2,8,128]{5,4,3,2,1,0:T(8,128)(2,1)S(1)}, u32[]{:S(2)}, u32[]{:S(2)}) collective-permute-start(bf16[8,16,2,2,8,128]{5,4,3,2,1,0:T(8,128)(2,1)S(1)} %bitcast.15), channel_id=1, source_target_pairs={{0,16},{16,0},{1,17},{17,1},{2,18},{18,2},{3,19},{19,3},{4,20},{20... | collective-permute-start | bytes 3145736 | tf_op jit(solution)/shard_map/ppermute | solution.py:370
  73.7 7.7 %collective-permute-start.1 = (bf16[8,16,2,2,8,128]{5,4,3,2,1,0:T(8,128)(2,1)S(1)}, bf16[8,16,2,2,8,128]{5,4,3,2,1,0:T(8,128)(2,1)S(1)}, u32[]{:S(2)}, u32[]{:S(2)}) collective-permute-start(bf16[8,16,2,2,8,128]{5,4,3,2,1,0:T(8,128)(2,1)S(1)} %get-tuple-element.25), channel_id=1, source_target_pairs={{0,16},{16,0},{1,17},{17,1},{2,18},{18,2},{3,19},{19,3},{4,20},{20... | collective-permute-start | bytes 3145736 | tf_op jit(solution)/shard_map/ppermute | solution.py:376

commit v4 on v3

--- a/solution.py
+++ b/solution.py
@@ -44,9 +44,9 @@
 
 
 def block_of(ref, index, which):
-    runs, _, slices, _, grain, _ = ref.shape
+    runs, _, slices, _, _, grain, _ = ref.shape
     parts = [
-        ref[:, 2 * index + u, :, which].astype(F32).reshape(runs * slices * grain, HD)
+        ref[:, index, :, u, which].astype(F32).reshape(runs * slices * grain, HD)
         for u in range(2)
     ]
     return jnp.concatenate(parts, axis=0).astype(BF16)
@@ -58,7 +58,7 @@
 
 def forward(keys_ref, parity, stretches, qt_ref, s_ref, e_ref, acc_ref):
     rows, cols = s_ref.shape[1:]
-    blocks = keys_ref.shape[1] // 2
+    blocks = keys_ref.shape[1]
     half = rows // 2
     heads = cols // half
     counts = counts_of(stretches, parity)
@@ -127,16 +127,15 @@
 
 
 def backward(keys_ref, parity, stretches, qt_ref, gt_ref, delta_ref, e_ref, acc_ref, out_ref):
-    runs, pairs, slices, _, grain, _ = keys_ref.shape
+    runs, blocks, slices, _, _, grain, _ = keys_ref.shape
     heads = qt_ref.shape[0] // 2
     half = runs * slices * grain
-    blocks = pairs // 2
     counts = counts_of(stretches, parity)
 
     def store(index, which, value):
         for u in range(2):
             part = value[u * half : (u + 1) * half].reshape(runs, slices, grain, HD)
-            out_ref[:, 2 * index + u, :, which] = part.astype(BF16)
+            out_ref[:, index, :, u, which] = part.astype(BF16)
 
     def pull(index, both):
         keys = block_of(keys_ref, index, 0)
@@ -298,7 +297,7 @@
     rows, width = queries.shape
     half = rows // 2
     cols = width // HD * half
-    slots = keys.shape[1] // 2 + keys.shape[1] // 4
+    slots = keys.shape[1] + keys.shape[1] // 2
     heads = cols // half
     return dict(
         weights=((slots, heads, 2 * half, half), BF16),
@@ -349,24 +348,27 @@
 
 
 AXES = ("zl", "xh", "xl", "core", "y", "zh")
-SPREAD = ("y", "zl", "xh", "xl", "zh")
+SPREAD = ("y", "zl", "xh", "zh")
 SWAP = ((0, 1), (1, 0))
 
 
 def per_device(queries, key_vectors, value_vectors, out_grads, pair_order):
     sizes = {name: lax.axis_size(name) for name in AXES}
-    runs, zl, xh, xl, zh = (sizes[name] for name in SPREAD)
+    runs, zl, xh, zh = (sizes[name] for name in SPREAD)
     rows = key_vectors.shape[0]
     kv_heads = key_vectors.shape[1] // HD
-    pairs = zl * xh * xl
     block = (2, rows, HD)
+    right = lax.axis_index("xl") == 1
 
     both = jnp.stack([key_vectors, value_vectors]).reshape(2, rows, kv_heads, HD)
-    sent = both.transpose(2, 0, 1, 3).reshape((1, zl, xh, 1, 1) + block)
-    sent = jnp.broadcast_to(sent, (runs, zl, xh, xl, zh) + block)
-    sent = sent.reshape((runs * pairs * zh,) + block)
+    both = both.transpose(2, 0, 1, 3)
+    near = lax.ppermute(both, "xl", SWAP)
+    sent = jnp.stack([jnp.where(right, near, both), jnp.where(right, both, near)], 1)
+    sent = sent.reshape((1, zl * xh, 1, 2) + block)
+    sent = jnp.broadcast_to(sent, (runs, zl * xh, zh, 2) + block)
+    sent = sent.reshape((runs * zl * xh * zh, 2) + block)
     mine = lax.all_to_all(sent, SPREAD, split_axis=0, concat_axis=0, tiled=True)
-    mine = mine.reshape((runs, pairs, zh) + block)
+    mine = mine.reshape((runs, zl * xh, zh, 2) + block)
     theirs = lax.ppermute(mine, "core", SWAP)
 
     qt, weights, acc, stat = attend_mine(pair_order, queries, mine)
@@ -378,10 +380,13 @@
         pair_order, queries, mine, qt, gt, delta, weights, acc
     )
     total = (dmine.astype(F32) + other.astype(F32)).astype(BF16)
-    total = total.reshape((runs * pairs * zh,) + block)
+    total = total.reshape((runs * zl * xh * zh, 2) + block)
     got = lax.all_to_all(total, SPREAD, split_axis=0, concat_axis=0, tiled=True)
-    got = got.reshape((runs, kv_heads, xl * zh) + block)
+    got = got.reshape((runs, kv_heads, zh, 2) + block)
     total = got.astype(F32).sum(axis=(0, 2))
+    own = jnp.where(right, total[:, 1], total[:, 0])
+    away = jnp.where(right, total[:, 0], total[:, 1]).astype(BF16)
+    total = own + lax.ppermute(away, "xl", SWAP).astype(F32)
     total = total.transpose(1, 2, 0, 3).reshape(2, rows, kv_heads * HD)
     return attended, query_grads, total[0], total[1]
 

time: 123 us -> 131 us (1.065)
  starting transfers between devices: 7.02 us -> 13.3 us
  waiting for transfers between devices: 0.01 us -> 3.73 us
    ppermute x0 -> x2, starting transfers between devices: none -> 6.13 us  [the longest x1 3.93 us: per_device(): near = lax.ppermute(both, 'xl', SWAP)]
    ppermute x0 -> x2, waiting for transfers between devices: none -> 3.73 us  [the longest x1 2.44 us: per_device(): total = own + lax.ppermute(away, 'xl', SWAP).astype(F32)]
    all_to_all x1, blocking collectives: 51.5 us -> 50 us  [per_device(): mine = lax.all_to_all(sent, SPREAD, split_axis=0, concat_axis=0, tiled=True)]
  transfers between devices with their start and end apart: 2 -> 4, of which waited for: 0 -> 2; matrix products, arithmetic and copies ran while one was open for 0% -> 0% of each run, Pallas kernels for 9% -> 8%
where the time goes in v4:
time: 131 us; the launch traced here: 129 us
  blocking collectives  88.6 us (68%)
  Pallas kernels  20 us (15%)
  starting transfers between devices  13.3 us (10%)
  waiting for transfers between devices  3.73 us (3%)
  other arithmetic  2.13 us (2%)
    all_to_all x1, blocking collectives, per_device(): mine = lax.all_to_all(sent, SPREAD, split_axis=0, concat_axis=0, tiled=True)  50 us
    all_to_all x1, blocking collectives, per_device(): got = lax.all_to_all(total, SPREAD, split_axis=0, concat_axis=0, tiled=True)  38.5 us
    pallas_call x3, Pallas kernels, call(): pl.pallas_call(kernel, out_shape=tuple((jax.ShapeDtypeStruct(*out) for ou...  20 us
    ppermute x1, starting transfers between devices, per_device(): theirs = lax.ppermute(mine, 'core', SWAP)  5.31 us
    ppermute x1, starting transfers between devices, per_device(): near = lax.ppermute(both, 'xl', SWAP)  3.93 us
  transfers between devices with their start and end apart: 4, of which 2 were waited for; matrix products, arithmetic and copies ran while one was open for 0% of the time, Pallas kernels for 8%

profile of v4, /device:TPU:1, one launch (start us, length us, event | category | flops | bytes accessed | tf_op | source)
XLA Modules:
  0.0 129.4 jit_solution(18153499199840976370)
XLA Ops:
  0.6 0.0 copy-start.2
  0.6 0.0 copy-start
  0.7 0.8 maximum_bitcast_fusion
  1.4 3.9 %collective-permute-start = (bf16[8,2,8,128]{3,2,0,1:T(8,128)(2,1)S(1)}, bf16[8,2,8,128]{3,2,0,1:T(8,128)(2,1)S(1)}, u32[]{:S(2)}, u32[]{:S(2)}) collective-permute-start(bf16[8,2,8,128]{3,2,0,1:T(8,128)(2,1)S(1)} %maximum_bitcast_fusion), channel_id=1, source_target_pairs={{0,32},{32,0},{1,33},{33,1},{2,34},{34,2},{3,35},{35,3},{4,36},{36... | collective-permute-start | bytes 98312 | tf_op jit(solution)/shard_map/ppermute | solution.py:365
  5.4 1.3 collective-permute-done
  6.7 0.7 select_bitcast_fusion.1
  7.4 0.2 broadcast_in_dim.2
  7.7 50.0 %all_to_all.10 = bf16[128,2,2,8,128]{4,3,2,1,0:T(8,128)(2,1)S(1)} all-to-all(bf16[128,2,2,8,128]{4,3,2,1,0:T(8,128)(2,1)S(1)} %bitcast.51), channel_id=1, replica_groups=mesh['zl'=4,'xh'=2,'xl'=2,'core'=2,'y'=8,'zh'=2] {'y','zl','xh','zh'}, dimensions={0} | all-to-all | bytes 2097152 | tf_op jit(solution)/shard_map/all_to_all | solution.py:370
  57.7 0.0 copy-start.1
  57.7 5.3 %collective-permute-start.1 = (bf16[8,8,2,2,2,8,128]{6,5,4,3,2,1,0:T(8,128)(2,1)S(1)}, bf16[8,8,2,2,2,8,128]{6,5,4,3,2,1,0:T(8,128)(2,1)S(1)}, u32[]{:S(2)}, u32[]{:S(2)}) collective-permute-start(bf16[8,8,2,2,2,8,128]{6,5,4,3,2,1,0:T(8,128)(2,1)S(1)} %bitcast.47), channel_id=1, source_target_pairs={{0,16},{16,0},{1,17},{17,1},{2,18},{18,2},{3,19},{19,3},{4,20},{20... | collective-permute-start | bytes 3145736 | tf_op jit(solution)/shard_map/ppermute | solution.py:372
  63.0 0.0 copy-done.2
  63.0 0.0 copy-done
  63.0 4.6 %first.1 = (bf16[8,128,128]{2,1,0:T(8,128)(2,1)S(1)}, bf16[12,4,256,128]{3,2,1,0:T(8,128)(2,1)S(1)}, f32[2,128,512]{2,1,0:T(8,128)S(1)}, f32[4,1,512]{2,1,0:T(1,128)S(1)}) custom-call(s32[32]{0:T(128)S(1)} %copy-done.2, bf16[256,512]{1,0:T(8,128)(2,1)S(1)} %copy-done, bf16[8,8,2,2,2,8,128]{6,5,4,3,2,1,0:T(8,128)(2,1)S(1)} %bitcast.48), custom_call_target="tpu_custom_call" | custom-call | flops 3221225472 | bytes 8388608 | tf_op jit(solution)/shard_map/first/pallas_call | solution.py:282
  67.6 0.0 collective-permute-done.1.keys_ref
  67.6 0.0 copy-done.1
  67.6 10.2 %second.1 = (bf16[256,512]{1,0:T(8,128)(2,1)}, bf16[8,128,128]{2,1,0:T(8,128)(2,1)S(1)}, f32[2,1,512]{2,1,0:T(1,128)S(1)}, bf16[8,8,2,2,2,8,128]{6,5,4,3,2,1,0:T(8,128)(2,1)S(1)}, f32[2,128,512]{2,1,0:T(8,128)S(1)}) custom-call(s32[32]{0:T(128)S(1)} %copy-done.2, bf16[256,512]{1,0:T(8,128)(2,1)S(1)} %copy-done.1, ...), custom_call_target="tpu_custom_call" | custom-call | flops 6442450944 | bytes 8388608 | tf_op jit(solution)/shard_map/second/pallas_call | solution.py:282
  77.8 1.9 %collective-permute-start.2 = (bf16[8,8,2,2,2,8,128]{6,5,4,3,2,1,0:T(8,128)(2,1)S(1)}, bf16[8,8,2,2,2,8,128]{6,5,4,3,2,1,0:T(8,128)(2,1)S(1)}, u32[]{:S(2)}, u32[]{:S(2)}) collective-permute-start(bf16[8,8,2,2,2,8,128]{6,5,4,3,2,1,0:T(8,128)(2,1)S(1)} %get-tuple-element.25), channel_id=1, source_target_pairs={{0,16},{16,0},{1,17},{17,1},{2,18},{18,2},{3,19},{19,3},{4,20},{20... | collective-permute-start | bytes 3145736 | tf_op jit(solution)/shard_map/ppermute | solution.py:378
  79.7 5.2 %third.1 = (bf16[8,8,2,2,2,8,128]{6,5,4,3,2,1,0:T(8,128)(2,1)S(1)}, bf16[256,512]{1,0:T(8,128)(2,1)}) custom-call(s32[32]{0:T(128)S(1)} %copy-done.2, bf16[8,8,2,2,2,8,128]{6,5,4,3,2,1,0:T(8,128)(2,1)S(1)} %bitcast.49, bf16[8,128,128]{2,1,0:T(8,128)(2,1)S(1)} %get-tuple-element.15.qt_ref, bf16[8,128,128]{2,1,0:T(8,128)(2,1)S(1)} %get-tuple-element.19.gt_ref, ...), custom_call_target="tpu_custom_call" | custom-call | flops 4294967296 | bytes 8388608 | tf_op jit(solution)/shard_map/third/pallas_call | solution.py:282
  85.0 0.0 collective-permute-done.2
  85.0 0.4 add_convert_fusion
  85.4 38.5 %all_to_all.11 = bf16[128,2,2,8,128]{4,3,2,1,0:T(8,128)(2,1)S(1)} all-to-all(bf16[128,2,2,8,128]{4,3,2,1,0:T(8,128)(2,1)S(1)} %bitcast.50), channel_id=1, replica_groups=mesh['zl'=4,'xh'=2,'xl'=2,'core'=2,'y'=8,'zh'=2] {'y','zl','xh','zh'}, dimensions={0} | all-to-all | bytes 2097152 | tf_op jit(solution)/shard_map/all_to_all | solution.py:384
  123.9 0.2 convert_reduce_fusion
  124.1 2.2 %collective-permute-start.3 = (bf16[8,2,8,128]{3,2,1,0:T(8,128)(2,1)S(1)}, bf16[8,2,8,128]{3,2,1,0:T(8,128)(2,1)S(1)}, u32[]{:S(2)}, u32[]{:S(2)}) collective-permute-start(bf16[8,2,8,128]{3,2,1,0:T(8,128)(2,1)S(1)} %fusion.3), channel_id=1, source_target_pairs={{0,32},{32,0},{1,33},{33,1},{2,34},{34,2},{3,35},{35,3},{4,36},{36... | collective-permute-start | bytes 98312 | tf_op jit(solution)/shard_map/ppermute | solution.py:389
  126.3 2.4 %collective-permute-done.3 = bf16[8,2,8,128]{3,2,1,0:T(8,128)(2,1)S(1)} collective-permute-done((bf16[8,2,8,128]{3,2,1,0:T(8,128)(2,1)S(1)}, bf16[8,2,8,128]{3,2,1,0:T(8,128)(2,1)S(1)}, u32[]{:S(2)}, u32[]{:S(2)}) %collective-permute-start.3) | collective-permute-done | bytes 32800 | tf_op jit(solution)/shard_map/ppermute | solution.py:389
  128.8 0.6 slice_bitcast_fusion
  (4 shorter events, 0.0 us)
Async XLA Ops:
  0.6 62.4 %copy-start.2 = (s32[32]{0:T(128)S(1)}, s32[32]{0:T(128)}, u32[]{:S(2)}) copy-start(s32[32]{0:T(128)} %order_ref.5) | copy-start | bytes 388
  0.6 62.4 %copy-start = (bf16[256,512]{1,0:T(8,128)(2,1)S(1)}, bf16[256,512]{1,0:T(8,128)(2,1)}, u32[]{:S(2)}) copy-start(bf16[256,512]{1,0:T(8,128)(2,1)} %q_ref.1) | copy-start | bytes 786436
  1.4 5.2 %collective-permute-start = (bf16[8,2,8,128]{3,2,0,1:T(8,128)(2,1)S(1)}, bf16[8,2,8,128]{3,2,0,1:T(8,128)(2,1)S(1)}, u32[]{:S(2)}, u32[]{:S(2)}) collective-permute-start(bf16[8,2,8,128]{3,2,0,1:T(8,128)(2,1)S(1)} %maximum_bitcast_fusion), channel_id=1, source_target_pairs={{0,32},{32,0},{1,33},{33,1},{2,34},{34,2},{3,35},{35,3},{4,36},{36... | collective-permute-start | bytes 98312 | tf_op jit(solution)/shard_map/ppermute | solution.py:365
  57.7 9.9 %copy-start.1 = (bf16[256,512]{1,0:T(8,128)(2,1)S(1)}, bf16[256,512]{1,0:T(8,128)(2,1)}, u32[]{:S(2)}) copy-start(bf16[256,512]{1,0:T(8,128)(2,1)} %g_ref.1) | copy-start | bytes 786436
  57.7 9.9 %collective-permute-start.1 = (bf16[8,8,2,2,2,8,128]{6,5,4,3,2,1,0:T(8,128)(2,1)S(1)}, bf16[8,8,2,2,2,8,128]{6,5,4,3,2,1,0:T(8,128)(2,1)S(1)}, u32[]{:S(2)}, u32[]{:S(2)}) collective-permute-start(bf16[8,8,2,2,2,8,128]{6,5,4,3,2,1,0:T(8,128)(2,1)S(1)} %bitcast.47), channel_id=1, source_target_pairs={{0,16},{16,0},{1,17},{17,1},{2,18},{18,2},{3,19},{19,3},{4,20},{20... | collective-permute-start | bytes 3145736 | tf_op jit(solution)/shard_map/ppermute | solution.py:372
  77.8 7.2 %collective-permute-start.2 = (bf16[8,8,2,2,2,8,128]{6,5,4,3,2,1,0:T(8,128)(2,1)S(1)}, bf16[8,8,2,2,2,8,128]{6,5,4,3,2,1,0:T(8,128)(2,1)S(1)}, u32[]{:S(2)}, u32[]{:S(2)}) collective-permute-start(bf16[8,8,2,2,2,8,128]{6,5,4,3,2,1,0:T(8,128)(2,1)S(1)} %get-tuple-element.25), channel_id=1, source_target_pairs={{0,16},{16,0},{1,17},{17,1},{2,18},{18,2},{3,19},{19,3},{4,20},{20... | collective-permute-start | bytes 3145736 | tf_op jit(solution)/shard_map/ppermute | solution.py:378
  124.1 4.7 %collective-permute-start.3 = (bf16[8,2,8,128]{3,2,1,0:T(8,128)(2,1)S(1)}, bf16[8,2,8,128]{3,2,1,0:T(8,128)(2,1)S(1)}, u32[]{:S(2)}, u32[]{:S(2)}) collective-permute-start(bf16[8,2,8,128]{3,2,1,0:T(8,128)(2,1)S(1)} %fusion.3), channel_id=1, source_target_pairs={{0,32},{32,0},{1,33},{33,1},{2,34},{34,2},{3,35},{35,3},{4,36},{36... | collective-permute-start | bytes 98312 | tf_op jit(solution)/shard_map/ppermute | solution.py:389

commit v5 on v3

v5 whole, which is shorter than its diff:
```python
import math
import jax
import jax.numpy as jnp
from jax import lax
from jax.experimental import pallas as pl
from jax.experimental.pallas import tpu as pltpu
from jax.sharding import Mesh, PartitionSpec as P


HD = 128
BF16 = jnp.bfloat16
F32 = jnp.float32
SCALE = 1.0 / math.sqrt(HD)
RATE = SCALE * math.log2(math.e)
FILL = -1e30
VMEM_BYTES = 24 << 20
CHUNK = 64
GROUP = 4
EXTRA = 16


def dot(a, b, a_axis, b_axis):
    return lax.dot_general(
        a, b, (((a_axis,), (b_axis,)), ((), ())), preferred_element_type=F32
    )


def flip(x):
    return x.astype(F32).T


def stretches_of(order_ref, half):
    first = 2 * (lax.axis_index("y") * lax.axis_size("zh") + lax.axis_index("zh"))
    late = jnp.where(order_ref[first + 1] > order_ref[first], 1, 0)
    stretches = (order_ref[first + late], order_ref[first + 1 - late])
    offsets = (
        pl.multiple_of(late * half, half),
        pl.multiple_of((1 - late) * half, half),
    )
    return stretches, offsets


def counts_of(stretches, parity):
    seen = [lax.shift_right_logical(s - parity + 2, 1) for s in stretches]
    return tuple(jnp.maximum(lax.shift_right_logical(n + 1, 1), 1) for n in seen)


def block_of(ref, index, which):
    runs, _, slices, _, grain, _ = ref.shape
    parts = [
        ref[:, 2 * index + u, :, which].astype(F32).reshape(runs * slices * grain, HD)
        for u in range(2)
    ]
    return jnp.concatenate(parts, axis=0).astype(BF16)


def wide(ref, first, count):
    return jnp.concatenate([ref[first + k] for k in range(count)], axis=1)


def forward(keys_ref, parity, stretches, qt_ref, s_ref, e_ref, acc_ref):
    rows, cols = s_ref.shape[1:]
    blocks = keys_ref.shape[1] // 2
    half = rows // 2
    heads = cols // half
    counts = counts_of(stretches, parity)
    bases = (0, blocks)
    shifts = []
    for t in range(2):

        def score(index, peak, masked):
            keys = block_of(keys_ref, index, 0)
            peaks = []
            for c in range(0, heads, GROUP):
                span = slice(c * half, (c + GROUP) * half)
                s = dot(keys, wide(qt_ref, t * heads + c, GROUP), 1, 0)
                if masked:
                    j = lax.broadcasted_iota(jnp.int32, s.shape, 0)
                    r = lax.rem(lax.broadcasted_iota(jnp.int32, s.shape, 1), half)
                    j = j + jnp.where(j >= half, half, 0)
                    ahead = (4 * index + parity - stretches[t]) * half
                    s = jnp.where(j + ahead <= r, s, FILL)
                s = s * RATE
                s_ref[bases[t] + index, :, span] = s
                high = jnp.max(s.reshape(-1, 8, GROUP * half), axis=0)
                peaks.append(jnp.maximum(peak[:, span], high))
            return jnp.concatenate(peaks, axis=1)

        last = counts[t] - 1
        peak = jnp.full((8, cols), FILL, F32)
        peak = lax.fori_loop(0, last, lambda i, p: score(i, p, False), peak)
        peak = score(last, peak, True)
        shifts.append(jnp.max(peak, axis=0, keepdims=True))

    results = []
    for t in range(2):

        def weigh(index):
            slot = bases[t] + index
            for h in range(heads):
                span = slice(h * half, (h + 1) * half)
                shift = shifts[t][:, span]
                for start in range(0, rows, CHUNK):
                    chunk = slice(start, start + CHUNK)
                    e = jnp.exp2(s_ref[slot, chunk, span] - shift)
                    e_ref[slot, h, chunk] = e.astype(BF16)

        def attend(index):
            values = block_of(keys_ref, index, 1).T
            ones = jnp.ones((EXTRA, rows), BF16)
            lines = jnp.concatenate([values, ones], axis=0)
            weights = wide(e_ref.at[bases[t] + index], 0, heads)
            acc_ref[t] += dot(lines, weights, 1, 0)

        acc_ref[t] = jnp.zeros(acc_ref.shape[1:], F32)
        weigh(0)

        @pl.loop(1, counts[t])
        def _(index):
            attend(index - 1)
            weigh(index)

        attend(counts[t] - 1)
        results.append((shifts[t], acc_ref[t, HD : HD + 1]))
    return results


def backward(keys_ref, parity, stretches, qt_ref, gt_ref, delta_ref, e_ref, out_ref):
    runs, pairs, slices, _, grain, _ = keys_ref.shape
    heads = qt_ref.shape[0] // 2
    half = runs * slices * grain
    blocks = pairs // 2
    counts = counts_of(stretches, parity)

    def store(index, which, value):
        for u in range(2):
            part = value[u * half : (u + 1) * half].reshape(runs, slices, grain, HD)
            out_ref[:, 2 * index + u, :, which] = part.astype(BF16)

    def pull(index, both):
        values = block_of(keys_ref, index, 1)
        key_term = value_term = 0.0
        for t in range(2 if both else 1):
            slot = index if t == 0 else blocks + index
            weights = wide(e_ref.at[slot], 0, heads)
            grads = wide(gt_ref, t * heads, heads)
            slope = dot(values, grads, 1, 0)
            parts = []
            for h in range(heads):
                span = slice(h * half, (h + 1) * half)
                part = e_ref[slot, h].astype(F32) * (slope[:, span] - delta_ref[t, :, span])
                parts.append(part.astype(BF16))
            ds = jnp.concatenate(parts, axis=1)
            value_term = value_term + dot(grads, weights, 1, 1)
            key_term = key_term + dot(wide(qt_ref, t * heads, heads), ds, 1, 1)
        store(index, 0, (key_term * SCALE).T)
        store(index, 1, value_term.T)

    @pl.loop(0, counts[1])
    def _(index):
        pull(index, True)

    @pl.loop(counts[1], counts[0])
    def _(index):
        pull(index, False)

    @pl.loop(counts[0], blocks)
    def _(index):
        for which in range(2):
            store(index, which, jnp.zeros((2 * half, HD), F32))


def prepare_kernel(order_ref, q_ref, g_ref, qt_ref, gt_ref):
    half = q_ref.shape[0] // 2
    heads = q_ref.shape[1] // HD
    _, offsets = stretches_of(order_ref, half)
    for t in range(2):
        for h in range(heads):
            rows, column = pl.ds(offsets[t], half), slice(h * HD, (h + 1) * HD)
            qt_ref[t * heads + h] = flip(q_ref[rows, column]).astype(BF16)
            gt_ref[t * heads + h] = flip(g_ref[rows, column]).astype(BF16)


def first_kernel(order_ref, keys_ref, qt_ref, e_ref, acc_ref, stat_ref, s_ref):
    stretches, _ = stretches_of(order_ref, s_ref.shape[1] // 2)
    parity = lax.axis_index("core")
    results = forward(keys_ref, parity, stretches, qt_ref, s_ref, e_ref, acc_ref)
    for t in range(2):
        for k in range(2):
            stat_ref[2 * t + k] = results[t][k]


def second_kernel(
    order_ref,
    keys_ref,
    qt_ref,
    g_ref,
    old_acc_ref,
    old_stat_ref,
    out_ref,
    gt_ref,
    delta_ref,
    own_gt_ref,
    own_delta_ref,
    shift_ref,
    dkeys_ref,
    s_ref,
    e_ref,
    acc_ref,
):
    half = s_ref.shape[1] // 2
    heads = g_ref.shape[0] // 2
    stretches, _ = stretches_of(order_ref, half)
    parity = 1 - lax.axis_index("core")
    results = forward(keys_ref, parity, stretches, qt_ref, s_ref, e_ref, acc_ref)
    for t in range(2):
        old_shift, old_total = old_stat_ref[2 * t], old_stat_ref[2 * t + 1]
        new_shift, new_total = results[t]
        shift_ref[t] = new_shift
        shift = jnp.maximum(old_shift, new_shift)
        old_part = jnp.exp2(old_shift - shift)
        new_part = jnp.exp2(new_shift - shift)
        inverse = 1.0 / (old_total * old_part + new_total * new_part)
        old_part = old_part * inverse
        new_part = new_part * inverse
        for h in range(heads):
            part = slice(h * half, (h + 1) * half)
            panel = t * heads + h
            total = old_acc_ref[t, :HD, part] * old_part[:, part]
            total = total + acc_ref[t, :HD, part] * new_part[:, part]
            out = total.astype(BF16)
            out_ref[panel] = out
            grad = g_ref[panel].astype(F32)
            gt_ref[panel] = (grad * old_part[:, part]).astype(BF16)
            own_gt_ref[panel] = (grad * new_part[:, part]).astype(BF16)
            delta = jnp.sum(grad * out.astype(F32), axis=0, keepdims=True)
            delta_ref[t, :, part] = delta * old_part[:, part]
            own_delta_ref[t, :, part] = delta * new_part[:, part]
    backward(
        keys_ref,
        parity,
        stretches,
        qt_ref,
        own_gt_ref,
        own_delta_ref,
        e_ref,
        dkeys_ref,
    )


def third_kernel(order_ref, keys_ref, qt_ref, gt_ref, delta_ref, e_ref, dkeys_ref):
    stretches, _ = stretches_of(order_ref, e_ref.shape[2] // 2)
    parity = lax.axis_index("core")
    backward(
        keys_ref, parity, stretches, qt_ref, gt_ref, delta_ref, e_ref, dkeys_ref
    )


def last_kernel(
    order_ref,
    mine_ref,
    theirs_ref,
    qt_ref,
    gt_ref,
    own_gt_ref,
    delta_ref,
    own_delta_ref,
    stat_ref,
    shift_ref,
    out_t_ref,
    out_ref,
    dq_ref,
    acc_ref,
):
    half = dq_ref.shape[0] // 2
    heads = dq_ref.shape[1] // HD
    stretches, offsets = stretches_of(order_ref, half)
    core = lax.axis_index("core")
    acc_ref[...] = jnp.zeros(acc_ref.shape, F32)

    def add(t, keys_ref, parity, panels_ref, row_ref, shift, index):
        keys = block_of(keys_ref, index, 0)
        values = block_of(keys_ref, index, 1)
        s = dot(keys, wide(qt_ref, t * heads, heads), 1, 0)
        j = lax.broadcasted_iota(jnp.int32, s.shape, 0)
        r = lax.rem(lax.broadcasted_iota(jnp.int32, s.shape, 1), half)
        j = j + jnp.where(j >= half, half, 0)
        ahead = (4 * index + parity - stretches[t]) * half
        s = jnp.where(j + ahead <= r, s, FILL) * RATE
        e = jnp.exp2(s - shift).astype(BF16).astype(F32)
        slope = dot(values, wide(panels_ref, t * heads, heads), 1, 0) - row_ref[t]
        acc_ref[t] += dot(keys, (e * slope).astype(BF16), 0, 0)

    for t in range(2):
        shift = stat_ref[2 * t]

        @pl.loop(0, counts_of(stretches, core)[t])
        def _(index, t=t, shift=shift):
            add(t, mine_ref, core, gt_ref, delta_ref, shift, index)

        shift = shift_ref[t]

        @pl.loop(0, counts_of(stretches, 1 - core)[t])
        def _(index, t=t, shift=shift):
            add(t, theirs_ref, 1 - core, own_gt_ref, own_delta_ref, shift, index)

    for t in range(2):
        for h in range(heads):
            rows, column = pl.ds(offsets[t], half), slice(h * HD, (h + 1) * HD)
            value = acc_ref[t, :, h * half : (h + 1) * half] * SCALE
            dq_ref[rows, column] = value.T.astype(BF16)
            out_ref[rows, column] = flip(out_t_ref[t * heads + h]).astype(BF16)


def call(kernel, outs, scratch, flops, *args):
    vmem = pl.BlockSpec(memory_space=pltpu.VMEM)
    return pl.pallas_call(
        kernel,
        out_shape=tuple(jax.ShapeDtypeStruct(*out) for out in outs),
        in_specs=[pl.BlockSpec(memory_space=pltpu.SMEM)] + [vmem] * (len(args) - 1),
        out_specs=(vmem,) * len(outs),
        scratch_shapes=[pltpu.VMEM(*item) for item in scratch],
        compiler_params=pltpu.CompilerParams(vmem_limit_bytes=VMEM_BYTES),
        cost_estimate=pl.CostEstimate(
            flops=flops, bytes_accessed=8 << 20, transcendentals=0
        ),
    )(*args)


def shapes_of(queries, keys):
    rows, width = queries.shape
    half = rows // 2
    cols = width // HD * half
    slots = keys.shape[1] // 2 + keys.shape[1] // 4
    heads = cols // half
    return dict(
        weights=((slots, heads, 2 * half, half), BF16),
        scores=((slots, 2 * half, cols), F32),
        flat=((2 * heads, HD, half), BF16),
        acc=((2, HD, cols), F32),
        sums=((2, HD + EXTRA, cols), F32),
        row=((2, 1, cols), F32),
        stat=((4, 1, cols), F32),
        keys=(keys.shape, BF16),
        queries=(queries.shape, BF16),
    )


def prepare(order, queries, grads, keys):
    s = shapes_of(queries, keys)
    outs = (s["flat"], s["flat"])
    return call(prepare_kernel, outs, (), 1 << 28, order, queries, grads)


def attend_mine(order, queries, mine, qt):
    s = shapes_of(queries, mine)
    outs = (s["weights"], s["sums"], s["stat"])
    return call(first_kernel, outs, (s["scores"],), 3 << 30, order, mine, qt)


def attend_theirs(order, queries, theirs, qt, grads, acc, stat):
    s = shapes_of(queries, theirs)
    outs = (s["flat"], s["flat"], s["row"], s["flat"], s["row"], s["row"], s["keys"])
    scratch = (s["scores"], s["weights"], s["sums"])
    return call(
        second_kernel, outs, scratch, 6 << 30, order, theirs, qt, grads, acc, stat
    )


def finish_mine(order, queries, mine, qt, gt, delta, weights):
    s = shapes_of(queries, mine)
    outs = (s["keys"],)
    args = (order, mine, qt, gt, delta, weights)
    return call(third_kernel, outs, (), 4 << 30, *args)[0]


def finish_queries(order, queries, mine, *args):
    s = shapes_of(queries, mine)
    outs = (s["queries"], s["queries"])
    scratch = (s["acc"],)
    return call(last_kernel, outs, scratch, 6 << 30, order, mine, *args)


AXES = ("zl", "xh", "xl", "core", "y", "zh")
SPREAD = ("y", "zl", "xh", "xl", "zh")
SWAP = ((0, 1), (1, 0))


def per_device(queries, key_vectors, value_vectors, out_grads, pair_order):
    sizes = {name: lax.axis_size(name) for name in AXES}
    runs, zl, xh, xl, zh = (sizes[name] for name in SPREAD)
    rows = key_vectors.shape[0]
    kv_heads = key_vectors.shape[1] // HD
    pairs = zl * xh * xl
    block = (2, rows, HD)

    both = jnp.stack([key_vectors, value_vectors]).reshape(2, rows, kv_heads, HD)
    sent = both.transpose(2, 0, 1, 3).reshape((1, zl, xh, 1, 1) + block)
    sent = jnp.broadcast_to(sent, (runs, zl, xh, xl, zh) + block)
    sent = sent.reshape((runs * pairs * zh,) + block)
    mine = lax.all_to_all(sent, SPREAD, split_axis=0, concat_axis=0, tiled=True)
    shape = jax.ShapeDtypeStruct((runs, pairs, zh) + block, BF16)
    qt, grads = prepare(pair_order, queries, out_grads, shape)
    mine = mine.reshape((runs, pairs, zh) + block)
    theirs = lax.ppermute(mine, "core", SWAP)

    weights, acc, stat = attend_mine(pair_order, queries, mine, qt)
    out_t, gt, delta, own_gt, own_delta, shift, dtheirs = attend_theirs(
        pair_order, queries, theirs, qt, grads, acc, stat
    )
    other = lax.ppermute(dtheirs, "core", SWAP)
    dmine = finish_mine(pair_order, queries, mine, qt, gt, delta, weights)
    total = (dmine.astype(F32) + other.astype(F32)).astype(BF16)
    total = total.reshape((runs * pairs * zh,) + block)
    got = lax.all_to_all(total, SPREAD, split_axis=0, concat_axis=0, tiled=True)
    got = got.reshape((runs, kv_heads, xl * zh) + block)
    total = got.astype(F32).sum(axis=(0, 2))
    total = total.transpose(1, 2, 0, 3).reshape(2, rows, kv_heads * HD)
    panels = (qt, gt, own_gt, delta, own_delta, stat, shift, out_t)
    attended, query_grads = finish_queries(pair_order, queries, mine, theirs, *panels)
    return attended, query_grads, total[0], total[1]


def solution(mesh):
    fine = Mesh(mesh.devices.reshape(4, 2, 2, 2, 8, 2), AXES)
    fsdp, cp = AXES[:4], AXES[4:]
    return jax.shard_map(
        per_device,
        mesh=fine,
        in_specs=(P(cp, fsdp), P(AXES, None), P(AXES, None), P(cp, fsdp), P()),
        out_specs=(P(cp, fsdp), P(cp, fsdp), P(AXES, None), P(AXES, None)),
        check_vma=False,
    )
```

time: 123 us -> 124 us (level)
  blocking collectives: 89.8 us -> 51.5 us
  waiting for transfers between devices: 0.01 us -> 18.3 us
  starting transfers between devices: 7.02 us -> 19.8 us
  Pallas kernels: 21.1 us -> 26.9 us
  other arithmetic: 1.22 us -> 3.54 us
    all_to_all x1 -> x0, blocking collectives: 38.2 us -> none  [per_device(): got = lax.all_to_all(total, SPREAD, split_axis=0, concat_axis=0, tiled=True)]
    all_to_all x0 -> x1, waiting for transfers between devices: none -> 18.3 us  [per_device(): got = lax.all_to_all(total, SPREAD, split_axis=0, concat_axis=0, tiled=True)]
    all_to_all x0 -> x1, starting transfers between devices: none -> 12.9 us  [per_device(): got = lax.all_to_all(total, SPREAD, split_axis=0, concat_axis=0, tiled=True)]
    pallas_call x3 -> x5, Pallas kernels: 21.1 us -> 26.9 us  [call(): pl.pallas_call(kernel, out_shape=tuple((jax.ShapeDtypeStruct(*out) for ou...]
  transfers between devices with their start and end apart: 2 -> 3, of which waited for: 0 -> 1; matrix products, arithmetic and copies ran while one was open for 0% -> 0% of each run, Pallas kernels for 9% -> 15%
where the time goes in v5:
time: 124 us; the launch traced here: 122 us
  blocking collectives  51.5 us (42%)
  Pallas kernels  26.9 us (22%)
  starting transfers between devices  19.8 us (16%)
  waiting for transfers between devices  18.3 us (15%)
  other arithmetic  3.54 us (3%)
    all_to_all x1, blocking collectives, per_device(): mine = lax.all_to_all(sent, SPREAD, split_axis=0, concat_axis=0, tiled=True)  51.5 us
    pallas_call x5, Pallas kernels, call(): pl.pallas_call(kernel, out_shape=tuple((jax.ShapeDtypeStruct(*out) for ou...  26.9 us
    all_to_all x1, waiting for transfers between devices, per_device(): got = lax.all_to_all(total, SPREAD, split_axis=0, concat_axis=0, tiled=True)  18.3 us
    all_to_all x1, starting transfers between devices, per_device(): got = lax.all_to_all(total, SPREAD, split_axis=0, concat_axis=0, tiled=True)  12.9 us
    ppermute x1, starting transfers between devices, per_device(): theirs = lax.ppermute(mine, 'core', SWAP)  4.97 us
  transfers between devices with their start and end apart: 3, of which 1 were waited for; matrix products, arithmetic and copies ran while one was open for 0% of the time, Pallas kernels for 15%

profile of v5, /device:TPU:1, one launch (start us, length us, event | category | flops | bytes accessed | tf_op | source)
XLA Modules:
  0.0 121.7 jit_solution(7722014830124781235)
XLA Ops:
  0.6 0.0 copy-start.2
  0.6 0.0 copy-start
  0.7 0.0 copy-start.1
  0.7 0.8 pad_maximum_fusion
  1.5 0.2 broadcast_in_dim.8
  1.7 51.5 %all_to_all.10 = bf16[256,2,8,128]{3,2,1,0:T(8,128)(2,1)S(1)} all-to-all(bf16[256,2,8,128]{3,2,1,0:T(8,128)(2,1)S(1)} %bitcast.20), channel_id=1, replica_groups=mesh['zl'=4,'xh'=2,'xl'=2,'core'=2,'y'=8,'zh'=2] {'y','zl','xh','xl','zh'}, dimensions={0} | all-to-all | bytes 2097152 | tf_op jit(solution)/shard_map/all_to_all | solution.py:401
  53.2 5.0 %collective-permute-start = (bf16[8,16,2,2,8,128]{5,4,3,2,1,0:T(8,128)(2,1)S(1)}, bf16[8,16,2,2,8,128]{5,4,3,2,1,0:T(8,128)(2,1)S(1)}, u32[]{:S(2)}, u32[]{:S(2)}) collective-permute-start(bf16[8,16,2,2,8,128]{5,4,3,2,1,0:T(8,128)(2,1)S(1)} %bitcast.15), channel_id=1, source_target_pairs={{0,16},{16,0},{1,17},{17,1},{2,18},{18,2},{3,19},{19,3},{4,20},{20... | collective-permute-start | bytes 3145736 | tf_op jit(solution)/shard_map/ppermute | solution.py:405
  58.2 0.0 copy-done.2
  58.2 0.0 copy-done
  58.2 0.0 copy-done.1
  58.2 0.8 shard_map.84
  59.0 4.3 %shard_map.85 = (bf16[12,4,256,128]{3,2,1,0:T(8,128)(2,1)S(1)}, f32[2,144,512]{2,1,0:T(8,128)S(1)}, f32[4,1,512]{2,1,0:T(1,128)S(1)}) custom-call(s32[32]{0:T(128)S(1)} %copy-done.2, bf16[8,16,2,2,8,128]{5,4,3,2,1,0:T(8,128)(2,1)S(1)} %bitcast.16, bf16[8,128,128]{2,1,0:T(8,128)(2,1)S(1)} %get-tuple-element.18.qt_ref), custom_call_target="tpu_custom_call" | custom-call | flops 3221225472 | bytes 8388608 | tf_op jit(solution)/shard_map/pallas_call | solution.py:317
  63.3 0.0 collective-permute-done.keys_ref.theirs_ref
  63.3 8.5 %shard_map.86 = (bf16[8,128,128]{2,1,0:T(8,128)(2,1)S(1)}, bf16[8,128,128]{2,1,0:T(8,128)(2,1)S(1)}, f32[2,1,512]{2,1,0:T(1,128)S(1)}, bf16[8,128,128]{2,1,0:T(8...) custom-call(s32[32]{0:T(128)S(1)} %copy-done.2, ...), custom_call_target="tpu_custom_call" | custom-call | flops 6442450944 | bytes 8388608 | tf_op jit(solution)/shard_map/pallas_call | solution.py:317
  71.8 1.9 %collective-permute-start.1 = (bf16[8,16,2,2,8,128]{5,4,3,2,1,0:T(8,128)(2,1)S(1)}, bf16[8,16,2,2,8,128]{5,4,3,2,1,0:T(8,128)(2,1)S(1)}, u32[]{:S(2)}, u32[]{:S(2)}) collective-permute-start(bf16[8,16,2,2,8,128]{5,4,3,2,1,0:T(8,128)(2,1)S(1)} %get-tuple-element.31), channel_id=1, source_target_pairs={{0,16},{16,0},{1,17},{17,1},{2,18},{18,2},{3,19},{19,3},{4,20},{20... | collective-permute-start | bytes 3145736 | tf_op jit(solution)/shard_map/ppermute | solution.py:411
  73.7 3.9 %shard_map.88 = bf16[8,16,2,2,8,128]{5,4,3,2,1,0:T(8,128)(2,1)S(1)} custom-call(s32[32]{0:T(128)S(1)} %copy-done.2, bf16[8,16,2,2,8,128]{5,4,3,2,1,0:T(8,128)(2,1)S(1)} %bitcast.17, bf16[8,128,128]{2,1,0:T(8,128)(2,1)S(1)} %get-tuple-element.18.qt_ref, bf16[8,128,128]{2,1,0:T(8,128)(2,1)S(1)} %get-tuple-element.22.gt_ref, ...), custom_call_target="tpu_custom_call" | custom-call | flops 4294967296 | bytes 8388608 | tf_op jit(solution)/shard_map/pallas_call | solution.py:317
  77.6 0.0 collective-permute-done.1
  77.6 1.3 %add_convert_fusion = bf16[8,16,2,2,8,128]{5,4,3,2,1,0:T(8,128)(2,1)} fusion(bf16[8,16,2,2,8,128]{5,4,3,2,1,0:T(8,128)(2,1)S(1)} %collective-permute-done.1, bf16[8,16,2,2,8,128]{5,4,3,2,1,0:T(8,128)(2,1)S(1)} %shard_map.88), kind=kLoop, calls=%fused_computation.1 | loop fusion | flops 2097152 | bytes 3145728 | tf_op jit(solution)/shard_map/convert_element_type | solution.py:413
  78.9 12.9 %all-to-all-start.1 = ((bf16[256,2,8,128]{3,2,1,0:T(8,128)(2,1)}), bf16[256,2,8,128]{3,2,1,0:T(8,128)(2,1)}, u32[]{:S(2)}, u32[]{:S(2)}) async-start(bf16[256,2,8,128]{3,2,1,0:T(8,128)(2,1)} %bitcast.19), calls=%async_computation.1 | async-start | bytes 2097152 | tf_op jit(solution)/shard_map/all_to_all | solution.py:415
  91.9 9.5 %shard_map.87 = (bf16[256,512]{1,0:T(8,128)(2,1)}, bf16[256,512]{1,0:T(8,128)(2,1)}) custom-call(s32[32]{0:T(128)S(1)} %copy-done.2, bf16[8,16,2,2,8,128]{5,4,3,2,1,0:T(8,128)(2,1)S(1)} %bitcast.18, bf16[8,16,2,2,8,128]{5,4,3,2,1,0:T(8,128)(2,1)S(1)} %collective-permute-done.keys_ref.theirs_ref, bf16[8,128,128]{2,1,0:T(8,128)(2,1)S(1)} %get-tuple-element.18.qt_ref, ...), custom_call_target="tpu_custom_call" | custom-call | flops 6442450944 | bytes 8388608 | tf_op jit(solution)/shard_map/pallas_call | solution.py:317
  101.3 18.3 %all-to-all-done.1 = bf16[256,2,8,128]{3,2,1,0:T(8,128)(2,1)} async-done(((bf16[256,2,8,128]{3,2,1,0:T(8,128)(2,1)}), bf16[256,2,8,128]{3,2,1,0:T(8,128)(2,1)}, u32[]{:S(2)}, u32[]{:S(2)}) %all-to-all-start.1) | async-done | bytes 1048608 | tf_op jit(solution)/shard_map/all_to_all | solution.py:415
  119.6 1.4 %convert_reduce_fusion = f32[8,2,8,128]{3,2,1,0:T(8,128)S(1)} fusion(bf16[8,8,4,2,8,128]{5,4,3,2,1,0:T(8,128)(2,1)} %bitcast.12), kind=kLoop, calls=%fused_computation | loop fusion | flops 1032192 | bytes 1114112 | tf_op jit(solution)/shard_map/reduce_sum | solution.py:417
  121.0 0.6 slice_bitcast_fusion
  (1 shorter events, 0.0 us)
Async XLA Ops:
  0.6 57.6 %copy-start.2 = (s32[32]{0:T(128)S(1)}, s32[32]{0:T(128)}, u32[]{:S(2)}) copy-start(s32[32]{0:T(128)} %order_ref.9) | copy-start | bytes 388
  0.6 57.6 %copy-start = (bf16[256,512]{1,0:T(8,128)(2,1)S(1)}, bf16[256,512]{1,0:T(8,128)(2,1)}, u32[]{:S(2)}) copy-start(bf16[256,512]{1,0:T(8,128)(2,1)} %q_ref.1) | copy-start | bytes 786436
  0.7 57.6 %copy-start.1 = (bf16[256,512]{1,0:T(8,128)(2,1)S(1)}, bf16[256,512]{1,0:T(8,128)(2,1)}, u32[]{:S(2)}) copy-start(bf16[256,512]{1,0:T(8,128)(2,1)} %g_ref.1) | copy-start | bytes 786436
  53.2 10.1 %collective-permute-start = (bf16[8,16,2,2,8,128]{5,4,3,2,1,0:T(8,128)(2,1)S(1)}, bf16[8,16,2,2,8,128]{5,4,3,2,1,0:T(8,128)(2,1)S(1)}, u32[]{:S(2)}, u32[]{:S(2)}) collective-permute-start(bf16[8,16,2,2,8,128]{5,4,3,2,1,0:T(8,128)(2,1)S(1)} %bitcast.15), channel_id=1, source_target_pairs={{0,16},{16,0},{1,17},{17,1},{2,18},{18,2},{3,19},{19,3},{4,20},{20... | collective-permute-start | bytes 3145736 | tf_op jit(solution)/shard_map/ppermute | solution.py:405
  71.8 5.8 %collective-permute-start.1 = (bf16[8,16,2,2,8,128]{5,4,3,2,1,0:T(8,128)(2,1)S(1)}, bf16[8,16,2,2,8,128]{5,4,3,2,1,0:T(8,128)(2,1)S(1)}, u32[]{:S(2)}, u32[]{:S(2)}) collective-permute-start(bf16[8,16,2,2,8,128]{5,4,3,2,1,0:T(8,128)(2,1)S(1)} %get-tuple-element.31), channel_id=1, source_target_pairs={{0,16},{16,0},{1,17},{17,1},{2,18},{18,2},{3,19},{19,3},{4,20},{20... | collective-permute-start | bytes 3145736 | tf_op jit(solution)/shard_map/ppermute | solution.py:411
  78.9 40.7 %all-to-all-start.1 = ((bf16[256,2,8,128]{3,2,1,0:T(8,128)(2,1)}), bf16[256,2,8,128]{3,2,1,0:T(8,128)(2,1)}, u32[]{:S(2)}, u32[]{:S(2)}) async-start(bf16[256,2,8,128]{3,2,1,0:T(8,128)(2,1)} %bitcast.19), calls=%async_computation.1 | async-start | bytes 2097152 | tf_op jit(solution)/shard_map/all_to_all | solution.py:415

commit v6 on v3

--- a/solution.py
+++ b/solution.py
@@ -15,6 +15,7 @@
 VMEM_BYTES = 32 << 20
 CHUNK = 64
 GROUP = 4
+EXTRA = 16
 
 
 def dot(a, b, a_axis, b_axis):
@@ -78,6 +79,7 @@
                     j = j + jnp.where(j >= half, half, 0)
                     ahead = (4 * index + parity - stretches[t]) * half
                     s = jnp.where(j + ahead <= r, s, FILL)
+                s = s * RATE
                 s_ref[bases[t] + index, :, span] = s
                 high = jnp.max(s.reshape(-1, 8, GROUP * half), axis=0)
                 peaks.append(jnp.maximum(peak[:, span], high))
@@ -87,42 +89,38 @@
         peak = jnp.full((8, cols), FILL, F32)
         peak = lax.fori_loop(0, last, lambda i, p: score(i, p, False), peak)
         peak = score(last, peak, True)
-        shifts.append(jnp.max(peak, axis=0, keepdims=True) * RATE)
+        shifts.append(jnp.max(peak, axis=0, keepdims=True))
 
     results = []
     for t in range(2):
 
-        def weigh(index, total):
+        def weigh(index):
             slot = bases[t] + index
-            totals = []
             for h in range(heads):
                 span = slice(h * half, (h + 1) * half)
                 shift = shifts[t][:, span]
-                part = total[:, span]
                 for start in range(0, rows, CHUNK):
                     chunk = slice(start, start + CHUNK)
-                    e = jnp.exp2(s_ref[slot, chunk, span] * RATE - shift)
+                    e = jnp.exp2(s_ref[slot, chunk, span] - shift)
                     e_ref[slot, h, chunk] = e.astype(BF16)
-                    part = part + jnp.sum(e.reshape(-1, 8, half), axis=0)
-                totals.append(part)
-            return jnp.concatenate(totals, axis=1)
 
         def attend(index):
-            values = block_of(keys_ref, index, 1)
-            for c in range(0, heads, GROUP):
-                span = slice(c * half, (c + GROUP) * half)
-                weights = wide(e_ref.at[bases[t] + index], c, GROUP)
-                acc_ref[t, :, span] += dot(values, weights, 0, 0)
-
-        def step(index, total):
+            values = block_of(keys_ref, index, 1).T
+            ones = jnp.ones((EXTRA, rows), BF16)
+            lines = jnp.concatenate([values, ones], axis=0)
+            weights = wide(e_ref.at[bases[t] + index], 0, heads)
+            acc_ref[t] += dot(lines, weights, 1, 0)
+
+        acc_ref[t] = jnp.zeros(acc_ref.shape[1:], F32)
+        weigh(0)
+
+        @pl.loop(1, counts[t])
+        def _(index):
             attend(index - 1)
-            return weigh(index, total)
-
-        acc_ref[t] = jnp.zeros(acc_ref.shape[1:], F32)
-        total = weigh(0, jnp.zeros((8, cols), F32))
-        total = lax.fori_loop(1, counts[t], step, total)
+            weigh(index)
+
         attend(counts[t] - 1)
-        results.append((shifts[t], jnp.sum(total, axis=0, keepdims=True)))
+        results.append((shifts[t], acc_ref[t, HD : HD + 1]))
     return results
 
 
@@ -220,8 +218,8 @@
         for h in range(heads):
             part = slice(h * half, (h + 1) * half)
             column = slice(h * HD, (h + 1) * HD)
-            total = old_acc_ref[t, :, part] * old_part[:, part]
-            total = total + acc_ref[t, :, part] * new_part[:, part]
+            total = old_acc_ref[t, :HD, part] * old_part[:, part]
+            total = total + acc_ref[t, :HD, part] * new_part[:, part]
             out = total.astype(BF16)
             out_ref[pl.ds(offsets[t], half), column] = flip(out).astype(BF16)
             grad = flip(g_ref[pl.ds(offsets[t], half), column])
@@ -305,6 +303,7 @@
         scores=((slots, 2 * half, cols), F32),
         flat=((2 * heads, HD, half), BF16),
         acc=((2, HD, cols), F32),
+        sums=((2, HD + EXTRA, cols), F32),
         row=((2, 1, cols), F32),
         stat=((4, 1, cols), F32),
         keys=(keys.shape, BF16),
@@ -314,7 +313,7 @@
 
 def attend_mine(order, queries, mine):
     s = shapes_of(queries, mine)
-    outs = (s["flat"], s["weights"], s["acc"], s["stat"])
+    outs = (s["flat"], s["weights"], s["sums"], s["stat"])
     return call(
         first_kernel, "first", outs, (s["scores"],), 3 << 30, order, queries, mine
     )
@@ -323,7 +322,7 @@
 def attend_theirs(order, grads, theirs, qt, acc, stat):
     s = shapes_of(grads, theirs)
     outs = (s["queries"], s["flat"], s["row"], s["keys"], s["acc"])
-    scratch = (s["scores"], s["weights"], s["acc"], s["flat"], s["row"])
+    scratch = (s["scores"], s["weights"], s["sums"], s["flat"], s["row"])
     return call(
         second_kernel, "second", outs, scratch, 6 << 30, order, grads, theirs, qt, acc, stat
     )

time: 123 us -> 122 us (level)
  no operation moved by 1% of the time
where the time goes in v6:
time: 122 us; the launch traced here: 121 us
  blocking collectives  90 us (74%)
  Pallas kernels  20.8 us (17%)
  starting transfers between devices  7.01 us (6%)
  other arithmetic  1.22 us (1%)
    all_to_all x1, blocking collectives, per_device(): mine = lax.all_to_all(sent, SPREAD, split_axis=0, concat_axis=0, tiled=True)  51.5 us
    all_to_all x1, blocking collectives, per_device(): got = lax.all_to_all(total, SPREAD, split_axis=0, concat_axis=0, tiled=True)  38.4 us
    pallas_call x3, Pallas kernels, call(): pl.pallas_call(kernel, out_shape=tuple((jax.ShapeDtypeStruct(*out) for ou...  20.8 us
    ppermute x1, starting transfers between devices, per_device(): theirs = lax.ppermute(mine, 'core', SWAP)  5.1 us
  transfers between devices with their start and end apart: 2, of which 0 were waited for; matrix products, arithmetic and copies ran while one was open for 0% of the time, Pallas kernels for 9%

profile of v6, /device:TPU:1, one launch (start us, length us, event | category | flops | bytes accessed | tf_op | source)
XLA Modules:
  0.0 120.5 jit_solution(15542379579794239967)
XLA Ops:
  0.6 0.0 copy-start.2
  0.6 0.0 copy-start
  0.7 0.8 pad_maximum_fusion
  1.4 0.2 broadcast_in_dim.8
  1.7 51.5 %all_to_all.10 = bf16[256,2,8,128]{3,2,1,0:T(8,128)(2,1)S(1)} all-to-all(bf16[256,2,8,128]{3,2,1,0:T(8,128)(2,1)S(1)} %bitcast.19), channel_id=1, replica_groups=mesh['zl'=4,'xh'=2,'xl'=2,'core'=2,'y'=8,'zh'=2] {'y','zl','xh','xl','zh'}, dimensions={0} | all-to-all | bytes 2097152 | tf_op jit(solution)/shard_map/all_to_all | solution.py:367
  53.2 0.0 copy-start.1
  53.2 5.1 %collective-permute-start = (bf16[8,16,2,2,8,128]{5,4,3,2,1,0:T(8,128)(2,1)S(1)}, bf16[8,16,2,2,8,128]{5,4,3,2,1,0:T(8,128)(2,1)S(1)}, u32[]{:S(2)}, u32[]{:S(2)}) collective-permute-start(bf16[8,16,2,2,8,128]{5,4,3,2,1,0:T(8,128)(2,1)S(1)} %bitcast.15), channel_id=1, source_target_pairs={{0,16},{16,0},{1,17},{17,1},{2,18},{18,2},{3,19},{19,3},{4,20},{20... | collective-permute-start | bytes 3145736 | tf_op jit(solution)/shard_map/ppermute | solution.py:369
  58.3 0.0 copy-done.2
  58.3 0.0 copy-done
  58.3 5.0 %first.1 = (bf16[8,128,128]{2,1,0:T(8,128)(2,1)S(1)}, bf16[12,4,256,128]{3,2,1,0:T(8,128)(2,1)S(1)}, f32[2,144,512]{2,1,0:T(8,128)S(1)}, f32[4,1,512]{2,1,0:T(1,128)S(1)}) custom-call(s32[32]{0:T(128)S(1)} %copy-done.2, bf16[256,512]{1,0:T(8,128)(2,1)S(1)} %copy-done, bf16[8,16,2,2,8,128]{5,4,3,2,1,0:T(8,128)(2,1)S(1)} %bitcast.16), custom_call_target="tpu_custom_call" | custom-call | flops 3221225472 | bytes 8388608 | tf_op jit(solution)/shard_map/first/pallas_call | solution.py:281
  63.3 0.0 collective-permute-done.keys_ref
  63.3 0.0 copy-done.1
  63.3 10.0 %second.1 = (bf16[256,512]{1,0:T(8,128)(2,1)}, bf16[8,128,128]{2,1,0:T(8,128)(2,1)S(1)}, f32[2,1,512]{2,1,0:T(1,128)S(1)}, bf16[8,16,2,2,8,128]{5,4,3,2,1,0:T(8,128)(2,1)S(1)}, f32[2,128,512]{2,1,0:T(8,128)S(1)}) custom-call(s32[32]{0:T(128)S(1)} %copy-done.2, bf16[256,512]{1,0:T(8,128)(2,1)S(1)} %copy-done.1, ...), custom_call_target="tpu_custom_call" | custom-call | flops 6442450944 | bytes 8388608 | tf_op jit(solution)/shard_map/second/pallas_call | solution.py:281
  73.4 1.9 %collective-permute-start.1 = (bf16[8,16,2,2,8,128]{5,4,3,2,1,0:T(8,128)(2,1)S(1)}, bf16[8,16,2,2,8,128]{5,4,3,2,1,0:T(8,128)(2,1)S(1)}, u32[]{:S(2)}, u32[]{:S(2)}) collective-permute-start(bf16[8,16,2,2,8,128]{5,4,3,2,1,0:T(8,128)(2,1)S(1)} %get-tuple-element.25), channel_id=1, source_target_pairs={{0,16},{16,0},{1,17},{17,1},{2,18},{18,2},{3,19},{19,3},{4,20},{20... | collective-permute-start | bytes 3145736 | tf_op jit(solution)/shard_map/ppermute | solution.py:375
  75.3 5.7 %third.1 = (bf16[8,16,2,2,8,128]{5,4,3,2,1,0:T(8,128)(2,1)S(1)}, bf16[256,512]{1,0:T(8,128)(2,1)}) custom-call(s32[32]{0:T(128)S(1)} %copy-done.2, bf16[8,16,2,2,8,128]{5,4,3,2,1,0:T(8,128)(2,1)S(1)} %bitcast.17, bf16[8,128,128]{2,1,0:T(8,128)(2,1)S(1)} %get-tuple-element.15.qt_ref, bf16[8,128,128]{2,1,0:T(8,128)(2,1)S(1)} %get-tuple-element.19.gt_ref, ...), custom_call_target="tpu_custom_call" | custom-call | flops 4294967296 | bytes 8388608 | tf_op jit(solution)/shard_map/third/pallas_call | solution.py:281
  81.0 0.0 collective-permute-done.1
  81.0 0.3 add_convert_fusion
  81.3 38.4 %all_to_all.11 = bf16[256,2,8,128]{3,2,1,0:T(8,128)(2,1)S(1)} all-to-all(bf16[256,2,8,128]{3,2,1,0:T(8,128)(2,1)S(1)} %bitcast.18), channel_id=1, replica_groups=mesh['zl'=4,'xh'=2,'xl'=2,'core'=2,'y'=8,'zh'=2] {'y','zl','xh','xl','zh'}, dimensions={0} | all-to-all | bytes 2097152 | tf_op jit(solution)/shard_map/all_to_all | solution.py:381
  119.7 0.2 convert_reduce_fusion
  119.9 0.6 slice_bitcast_fusion
  (1 shorter events, 0.0 us)
Async XLA Ops:
  0.6 57.7 %copy-start.2 = (s32[32]{0:T(128)S(1)}, s32[32]{0:T(128)}, u32[]{:S(2)}) copy-start(s32[32]{0:T(128)} %order_ref.5) | copy-start | bytes 388
  0.6 57.7 %copy-start = (bf16[256,512]{1,0:T(8,128)(2,1)S(1)}, bf16[256,512]{1,0:T(8,128)(2,1)}, u32[]{:S(2)}) copy-start(bf16[256,512]{1,0:T(8,128)(2,1)} %q_ref.1) | copy-start | bytes 786436
  53.2 10.1 %copy-start.1 = (bf16[256,512]{1,0:T(8,128)(2,1)S(1)}, bf16[256,512]{1,0:T(8,128)(2,1)}, u32[]{:S(2)}) copy-start(bf16[256,512]{1,0:T(8,128)(2,1)} %g_ref.1) | copy-start | bytes 786436
  53.2 10.1 %collective-permute-start = (bf16[8,16,2,2,8,128]{5,4,3,2,1,0:T(8,128)(2,1)S(1)}, bf16[8,16,2,2,8,128]{5,4,3,2,1,0:T(8,128)(2,1)S(1)}, u32[]{:S(2)}, u32[]{:S(2)}) collective-permute-start(bf16[8,16,2,2,8,128]{5,4,3,2,1,0:T(8,128)(2,1)S(1)} %bitcast.15), channel_id=1, source_target_pairs={{0,16},{16,0},{1,17},{17,1},{2,18},{18,2},{3,19},{19,3},{4,20},{20... | collective-permute-start | bytes 3145736 | tf_op jit(solution)/shard_map/ppermute | solution.py:369
  73.4 7.7 %collective-permute-start.1 = (bf16[8,16,2,2,8,128]{5,4,3,2,1,0:T(8,128)(2,1)S(1)}, bf16[8,16,2,2,8,128]{5,4,3,2,1,0:T(8,128)(2,1)S(1)}, u32[]{:S(2)}, u32[]{:S(2)}) collective-permute-start(bf16[8,16,2,2,8,128]{5,4,3,2,1,0:T(8,128)(2,1)S(1)} %get-tuple-element.25), channel_id=1, source_target_pairs={{0,16},{16,0},{1,17},{17,1},{2,18},{18,2},{3,19},{19,3},{4,20},{20... | collective-permute-start | bytes 3145736 | tf_op jit(solution)/shard_map/ppermute | solution.py:375

commit v7 on v3

--- a/solution.py
+++ b/solution.py
@@ -364,7 +364,7 @@
     both = jnp.stack([key_vectors, value_vectors]).reshape(2, rows, kv_heads, HD)
     sent = both.transpose(2, 0, 1, 3).reshape((1, zl, xh, 1, 1) + block)
     sent = jnp.broadcast_to(sent, (runs, zl, xh, xl, zh) + block)
-    sent = sent.reshape((runs * pairs * zh,) + block)
+    sent = sent.reshape(runs * pairs * zh, 2 * rows, HD)
     mine = lax.all_to_all(sent, SPREAD, split_axis=0, concat_axis=0, tiled=True)
     mine = mine.reshape((runs, pairs, zh) + block)
     theirs = lax.ppermute(mine, "core", SWAP)
@@ -378,7 +378,7 @@
         pair_order, queries, mine, qt, gt, delta, weights, acc
     )
     total = (dmine.astype(F32) + other.astype(F32)).astype(BF16)
-    total = total.reshape((runs * pairs * zh,) + block)
+    total = total.reshape(runs * pairs * zh, 2 * rows, HD)
     got = lax.all_to_all(total, SPREAD, split_axis=0, concat_axis=0, tiled=True)
     got = got.reshape((runs, kv_heads, xl * zh) + block)
     total = got.astype(F32).sum(axis=(0, 2))

time: 123 us -> 123 us (level)
  no operation moved by 1% of the time
where the time goes in v7:
time: 123 us; the launch traced here: 121 us
  blocking collectives  89.6 us (73%)
  Pallas kernels  21.8 us (18%)
  starting transfers between devices  7.01 us (6%)
    all_to_all x1, blocking collectives, per_device(): mine = lax.all_to_all(sent, SPREAD, split_axis=0, concat_axis=0, tiled=True)  51.5 us
    all_to_all x1, blocking collectives, per_device(): got = lax.all_to_all(total, SPREAD, split_axis=0, concat_axis=0, tiled=True)  38 us
    pallas_call x3, Pallas kernels, call(): pl.pallas_call(kernel, out_shape=tuple((jax.ShapeDtypeStruct(*out) for ou...  21.8 us
    ppermute x1, starting transfers between devices, per_device(): theirs = lax.ppermute(mine, 'core', SWAP)  5.1 us
  transfers between devices with their start and end apart: 2, of which 0 were waited for; matrix products, arithmetic and copies ran while one was open for 0% of the time, Pallas kernels for 9%

profile of v7, /device:TPU:1, one launch (start us, length us, event | category | flops | bytes accessed | tf_op | source)
XLA Modules:
  0.0 121.2 jit_solution(18116791749396652829)
XLA Ops:
  0.6 0.0 copy-start.2
  0.6 0.0 copy-start
  0.7 0.8 pad_maximum_fusion
  1.4 0.2 broadcast_in_dim.8
  1.7 51.5 %all_to_all.10 = bf16[256,16,128]{2,1,0:T(8,128)(2,1)S(1)} all-to-all(bf16[256,16,128]{2,1,0:T(8,128)(2,1)S(1)} %bitcast.19), channel_id=1, replica_groups=mesh['zl'=4,'xh'=2,'xl'=2,'core'=2,'y'=8,'zh'=2] {'y','zl','xh','xl','zh'}, dimensions={0} | all-to-all | bytes 2097152 | tf_op jit(solution)/shard_map/all_to_all | solution.py:368
  53.2 0.0 copy-start.1
  53.2 5.1 %collective-permute-start = (bf16[8,16,2,2,8,128]{5,4,3,2,1,0:T(8,128)(2,1)S(1)}, bf16[8,16,2,2,8,128]{5,4,3,2,1,0:T(8,128)(2,1)S(1)}, u32[]{:S(2)}, u32[]{:S(2)}) collective-permute-start(bf16[8,16,2,2,8,128]{5,4,3,2,1,0:T(8,128)(2,1)S(1)} %bitcast.15), channel_id=1, source_target_pairs={{0,16},{16,0},{1,17},{17,1},{2,18},{18,2},{3,19},{19,3},{4,20},{20... | collective-permute-start | bytes 3145736 | tf_op jit(solution)/shard_map/ppermute | solution.py:370
  58.3 0.0 copy-done.2
  58.3 0.0 copy-done
  58.3 5.2 %first.1 = (bf16[8,128,128]{2,1,0:T(8,128)(2,1)S(1)}, bf16[12,4,256,128]{3,2,1,0:T(8,128)(2,1)S(1)}, f32[2,128,512]{2,1,0:T(8,128)S(1)}, f32[4,1,512]{2,1,0:T(1,128)S(1)}) custom-call(s32[32]{0:T(128)S(1)} %copy-done.2, bf16[256,512]{1,0:T(8,128)(2,1)S(1)} %copy-done, bf16[8,16,2,2,8,128]{5,4,3,2,1,0:T(8,128)(2,1)S(1)} %bitcast.16), custom_call_target="tpu_custom_call" | custom-call | flops 3221225472 | bytes 8388608 | tf_op jit(solution)/shard_map/first/pallas_call | solution.py:283
  63.5 0.0 collective-permute-done.keys_ref
  63.5 0.0 copy-done.1
  63.5 10.6 %second.1 = (bf16[256,512]{1,0:T(8,128)(2,1)}, bf16[8,128,128]{2,1,0:T(8,128)(2,1)S(1)}, f32[2,1,512]{2,1,0:T(1,128)S(1)}, bf16[8,16,2,2,8,128]{5,4,3,2,1,0:T(8,128)(2,1)S(1)}, f32[2,128,512]{2,1,0:T(8,128)S(1)}) custom-call(s32[32]{0:T(128)S(1)} %copy-done.2, bf16[256,512]{1,0:T(8,128)(2,1)S(1)} %copy-done.1, ...), custom_call_target="tpu_custom_call" | custom-call | flops 6442450944 | bytes 8388608 | tf_op jit(solution)/shard_map/second/pallas_call | solution.py:283
  74.1 1.9 %collective-permute-start.1 = (bf16[8,16,2,2,8,128]{5,4,3,2,1,0:T(8,128)(2,1)S(1)}, bf16[8,16,2,2,8,128]{5,4,3,2,1,0:T(8,128)(2,1)S(1)}, u32[]{:S(2)}, u32[]{:S(2)}) collective-permute-start(bf16[8,16,2,2,8,128]{5,4,3,2,1,0:T(8,128)(2,1)S(1)} %get-tuple-element.25), channel_id=1, source_target_pairs={{0,16},{16,0},{1,17},{17,1},{2,18},{18,2},{3,19},{19,3},{4,20},{20... | collective-permute-start | bytes 3145736 | tf_op jit(solution)/shard_map/ppermute | solution.py:376
  76.0 6.0 %third.1 = (bf16[8,16,2,2,8,128]{5,4,3,2,1,0:T(8,128)(2,1)S(1)}, bf16[256,512]{1,0:T(8,128)(2,1)}) custom-call(s32[32]{0:T(128)S(1)} %copy-done.2, bf16[8,16,2,2,8,128]{5,4,3,2,1,0:T(8,128)(2,1)S(1)} %bitcast.17, bf16[8,128,128]{2,1,0:T(8,128)(2,1)S(1)} %get-tuple-element.15.qt_ref, bf16[8,128,128]{2,1,0:T(8,128)(2,1)S(1)} %get-tuple-element.19.gt_ref, ...), custom_call_target="tpu_custom_call" | custom-call | flops 4294967296 | bytes 8388608 | tf_op jit(solution)/shard_map/third/pallas_call | solution.py:283
  82.0 0.0 collective-permute-done.1
  82.0 0.3 add_convert_fusion
  82.3 38.0 %all_to_all.11 = bf16[256,16,128]{2,1,0:T(8,128)(2,1)S(1)} all-to-all(bf16[256,16,128]{2,1,0:T(8,128)(2,1)S(1)} %bitcast.18), channel_id=1, replica_groups=mesh['zl'=4,'xh'=2,'xl'=2,'core'=2,'y'=8,'zh'=2] {'y','zl','xh','xl','zh'}, dimensions={0} | all-to-all | bytes 2097152 | tf_op jit(solution)/shard_map/all_to_all | solution.py:382
  120.4 0.2 convert_reduce_fusion
  120.5 0.6 slice_bitcast_fusion
  (1 shorter events, 0.0 us)
Async XLA Ops:
  0.6 57.7 %copy-start.2 = (s32[32]{0:T(128)S(1)}, s32[32]{0:T(128)}, u32[]{:S(2)}) copy-start(s32[32]{0:T(128)} %order_ref.5) | copy-start | bytes 388
  0.6 57.7 %copy-start = (bf16[256,512]{1,0:T(8,128)(2,1)S(1)}, bf16[256,512]{1,0:T(8,128)(2,1)}, u32[]{:S(2)}) copy-start(bf16[256,512]{1,0:T(8,128)(2,1)} %q_ref.1) | copy-start | bytes 786436
  53.2 10.3 %copy-start.1 = (bf16[256,512]{1,0:T(8,128)(2,1)S(1)}, bf16[256,512]{1,0:T(8,128)(2,1)}, u32[]{:S(2)}) copy-start(bf16[256,512]{1,0:T(8,128)(2,1)} %g_ref.1) | copy-start | bytes 786436
  53.2 10.3 %collective-permute-start = (bf16[8,16,2,2,8,128]{5,4,3,2,1,0:T(8,128)(2,1)S(1)}, bf16[8,16,2,2,8,128]{5,4,3,2,1,0:T(8,128)(2,1)S(1)}, u32[]{:S(2)}, u32[]{:S(2)}) collective-permute-start(bf16[8,16,2,2,8,128]{5,4,3,2,1,0:T(8,128)(2,1)S(1)} %bitcast.15), channel_id=1, source_target_pairs={{0,16},{16,0},{1,17},{17,1},{2,18},{18,2},{3,19},{19,3},{4,20},{20... | collective-permute-start | bytes 3145736 | tf_op jit(solution)/shard_map/ppermute | solution.py:370
  74.1 7.9 %collective-permute-start.1 = (bf16[8,16,2,2,8,128]{5,4,3,2,1,0:T(8,128)(2,1)S(1)}, bf16[8,16,2,2,8,128]{5,4,3,2,1,0:T(8,128)(2,1)S(1)}, u32[]{:S(2)}, u32[]{:S(2)}) collective-permute-start(bf16[8,16,2,2,8,128]{5,4,3,2,1,0:T(8,128)(2,1)S(1)} %get-tuple-element.25), channel_id=1, source_target_pairs={{0,16},{16,0},{1,17},{17,1},{2,18},{18,2},{3,19},{19,3},{4,20},{20... | collective-permute-start | bytes 3145736 | tf_op jit(solution)/shard_map/ppermute | solution.py:376

commit v8 on v3

--- a/solution.py
+++ b/solution.py
@@ -14,7 +14,6 @@
 FILL = -1e30
 VMEM_BYTES = 32 << 20
 CHUNK = 64
-GROUP = 4
 
 
 def dot(a, b, a_axis, b_axis):
@@ -63,108 +62,130 @@
     heads = cols // half
     counts = counts_of(stretches, parity)
     bases = (0, blocks)
-    shifts = []
-    for t in range(2):
-
-        def score(index, peak, masked):
-            keys = block_of(keys_ref, index, 0)
-            peaks = []
-            for c in range(0, heads, GROUP):
-                span = slice(c * half, (c + GROUP) * half)
-                s = dot(keys, wide(qt_ref, t * heads + c, GROUP), 1, 0)
-                if masked:
-                    j = lax.broadcasted_iota(jnp.int32, s.shape, 0)
-                    r = lax.rem(lax.broadcasted_iota(jnp.int32, s.shape, 1), half)
-                    j = j + jnp.where(j >= half, half, 0)
-                    ahead = (4 * index + parity - stretches[t]) * half
-                    s = jnp.where(j + ahead <= r, s, FILL)
-                s_ref[bases[t] + index, :, span] = s
-                high = jnp.max(s.reshape(-1, 8, GROUP * half), axis=0)
-                peaks.append(jnp.maximum(peak[:, span], high))
-            return jnp.concatenate(peaks, axis=1)
-
-        last = counts[t] - 1
-        peak = jnp.full((8, cols), FILL, F32)
-        peak = lax.fori_loop(0, last, lambda i, p: score(i, p, False), peak)
-        peak = score(last, peak, True)
-        shifts.append(jnp.max(peak, axis=0, keepdims=True) * RATE)
-
-    results = []
-    for t in range(2):
-
-        def weigh(index, total):
-            slot = bases[t] + index
-            totals = []
-            for h in range(heads):
-                span = slice(h * half, (h + 1) * half)
-                shift = shifts[t][:, span]
-                part = total[:, span]
-                for start in range(0, rows, CHUNK):
-                    chunk = slice(start, start + CHUNK)
-                    e = jnp.exp2(s_ref[slot, chunk, span] * RATE - shift)
-                    e_ref[slot, h, chunk] = e.astype(BF16)
-                    part = part + jnp.sum(e.reshape(-1, 8, half), axis=0)
-                totals.append(part)
-            return jnp.concatenate(totals, axis=1)
-
-        def attend(index):
-            values = block_of(keys_ref, index, 1)
-            for c in range(0, heads, GROUP):
-                span = slice(c * half, (c + GROUP) * half)
-                weights = wide(e_ref.at[bases[t] + index], c, GROUP)
-                acc_ref[t, :, span] += dot(values, weights, 0, 0)
-
-        def step(index, total):
-            attend(index - 1)
-            return weigh(index, total)
-
-        acc_ref[t] = jnp.zeros(acc_ref.shape[1:], F32)
-        total = weigh(0, jnp.zeros((8, cols), F32))
-        total = lax.fori_loop(1, counts[t], step, total)
-        attend(counts[t] - 1)
-        results.append((shifts[t], jnp.sum(total, axis=0, keepdims=True)))
-    return results
-
-
-def backward(keys_ref, parity, stretches, qt_ref, gt_ref, delta_ref, e_ref, acc_ref, out_ref):
+    long, short = counts
+
+    def score(t, index, peak, masked):
+        keys = block_of(keys_ref, index, 0)
+        s = dot(keys, wide(qt_ref, t * heads, heads), 1, 0)
+        if masked:
+            j = lax.broadcasted_iota(jnp.int32, s.shape, 0)
+            r = lax.rem(lax.broadcasted_iota(jnp.int32, s.shape, 1), half)
+            j = j + jnp.where(j >= half, half, 0)
+            ahead = (4 * index + parity - stretches[t]) * half
+            s = jnp.where(j + ahead <= r, s, FILL)
+        s_ref[bases[t] + index] = s
+        return jnp.maximum(peak, jnp.max(s.reshape(-1, 8, cols), axis=0))
+
+    def weigh(t, index, total):
+        slot = bases[t] + index
+        totals = []
+        for h in range(heads):
+            span = slice(h * half, (h + 1) * half)
+            part = total[:, span]
+            for start in range(0, rows, CHUNK):
+                chunk = slice(start, start + CHUNK)
+                e = jnp.exp2(s_ref[slot, chunk, span] * RATE - shifts[t][:, span])
+                e_ref[slot, h, chunk] = e.astype(BF16)
+                part = part + jnp.sum(e.reshape(-1, 8, half), axis=0)
+            totals.append(part)
+        return jnp.concatenate(totals, axis=1)
+
+    def attend(t, index):
+        values = block_of(keys_ref, index, 1)
+        weights = wide(e_ref.at[bases[t] + index], 0, heads)
+        acc_ref[t] += dot(values, weights, 0, 0)
+
+    def score_both(i, peaks):
+        return score(0, i, peaks[0], False), score(1, i, peaks[1], False)
+
+    peak = jnp.full((8, cols), FILL, F32)
+    peaks = lax.fori_loop(0, short - 1, score_both, (peak, peak))
+    first = lax.fori_loop(
+        short - 1, long - 1, lambda i, p: score(0, i, p, False), peaks[0]
+    )
+    peaks = (score(0, long - 1, first, True), score(1, short - 1, peaks[1], True))
+    shifts = [jnp.max(p, axis=0, keepdims=True) * RATE for p in peaks]
+
+    def step_both(i, totals):
+        for t in range(2):
+            attend(t, i - 1)
+        return weigh(0, i, totals[0]), weigh(1, i, totals[1])
+
+    def step_long(i, total):
+        attend(0, i - 1)
+        return weigh(0, i, total)
+
+    acc_ref[...] = jnp.zeros(acc_ref.shape, F32)
+    zero = jnp.zeros((8, cols), F32)
+    totals = (weigh(0, 0, zero), weigh(1, 0, zero))
+    totals = lax.fori_loop(1, short, step_both, totals)
+    last = lax.fori_loop(short, long, step_long, totals[0])
+    attend(1, short - 1)
+    attend(0, long - 1)
+    sums = [jnp.sum(x, axis=0, keepdims=True) for x in (last, totals[1])]
+    return list(zip(shifts, sums))
+
+
+def backward(
+    keys_ref, parity, stretches, qt_ref, gt_ref, delta_ref, e_ref, acc_ref, ds_ref, out_ref
+):
     runs, pairs, slices, _, grain, _ = keys_ref.shape
     heads = qt_ref.shape[0] // 2
     half = runs * slices * grain
     blocks = pairs // 2
-    counts = counts_of(stretches, parity)
+    long, short = counts_of(stretches, parity)
 
     def store(index, which, value):
         for u in range(2):
             part = value[u * half : (u + 1) * half].reshape(runs, slices, grain, HD)
             out_ref[:, 2 * index + u, :, which] = part.astype(BF16)
 
-    def pull(index, both):
+    def weights_of(t, index):
+        return wide(e_ref.at[index if t == 0 else blocks + index], 0, heads)
+
+    def slopes(index, both):
+        values = block_of(keys_ref, index, 1)
+        for t in range(2 if both else 1):
+            slope = dot(values, wide(gt_ref, t * heads, heads), 1, 0)
+            for h in range(heads):
+                span = slice(h * half, (h + 1) * half)
+                weight = e_ref[index if t == 0 else blocks + index, h].astype(F32)
+                part = weight * (slope[:, span] - delta_ref[t, :, span])
+                ds_ref[t * heads + h] = part.astype(BF16)
+
+    def finish(index, both):
         keys = block_of(keys_ref, index, 0)
-        values = block_of(keys_ref, index, 1)
         key_term = value_term = 0.0
         for t in range(2 if both else 1):
-            slot = index if t == 0 else blocks + index
-            for c in range(0, heads, GROUP):
-                span = slice(c * half, (c + GROUP) * half)
-                weights = wide(e_ref.at[slot], c, GROUP)
-                grads = wide(gt_ref, t * heads + c, GROUP)
-                slope = dot(values, grads, 1, 0) - delta_ref[t, :, span]
-                ds = (weights.astype(F32) * slope).astype(BF16)
-                value_term = value_term + dot(grads, weights, 1, 1)
-                key_term = key_term + dot(wide(qt_ref, t * heads + c, GROUP), ds, 1, 1)
-                acc_ref[t, :, span] += dot(keys, ds, 0, 0)
+            ds = wide(ds_ref, t * heads, heads)
+            grads = wide(gt_ref, t * heads, heads)
+            value_term = value_term + dot(grads, weights_of(t, index), 1, 1)
+            key_term = key_term + dot(wide(qt_ref, t * heads, heads), ds, 1, 1)
+            acc_ref[t] += dot(keys, ds, 0, 0)
         store(index, 0, (key_term * SCALE).T)
         store(index, 1, value_term.T)
 
-    @pl.loop(0, counts[1])
+    slopes(0, True)
+
+    @pl.loop(1, short)
     def _(index):
-        pull(index, True)
-
-    @pl.loop(counts[1], counts[0])
-    def _(index):
-        pull(index, False)
-
-    @pl.loop(counts[0], blocks)
+        finish(index - 1, True)
+        slopes(index, True)
+
+    finish(short - 1, True)
+
+    @pl.when(long > short)
+    def _():
+        slopes(short, False)
+
+        @pl.loop(short + 1, long)
+        def _(index):
+            finish(index - 1, False)
+            slopes(index, False)
+
+        finish(long - 1, False)
+
+    @pl.loop(long, blocks)
     def _(index):
         for which in range(2):
             store(index, which, jnp.zeros((2 * half, HD), F32))
@@ -202,6 +223,7 @@
     acc_ref,
     own_gt_ref,
     own_delta_ref,
+    ds_ref,
 ):
     half = g_ref.shape[0] // 2
     heads = g_ref.shape[1] // HD
@@ -240,6 +262,7 @@
         own_delta_ref,
         e_ref,
         dq_acc_ref,
+        ds_ref,
         dkeys_ref,
     )
 
@@ -255,6 +278,7 @@
     dkeys_ref,
     dq_ref,
     acc_ref,
+    ds_ref,
 ):
     half = dq_ref.shape[0] // 2
     heads = dq_ref.shape[1] // HD
@@ -270,6 +294,7 @@
         delta_ref,
         e_ref,
         acc_ref,
+        ds_ref,
         dkeys_ref,
     )
     for t in range(2):
@@ -305,6 +330,7 @@
         scores=((slots, 2 * half, cols), F32),
         flat=((2 * heads, HD, half), BF16),
         acc=((2, HD, cols), F32),
+        ds=((2 * heads, 2 * half, half), BF16),
         row=((2, 1, cols), F32),
         stat=((4, 1, cols), F32),
         keys=(keys.shape, BF16),
@@ -323,7 +349,7 @@
 def attend_theirs(order, grads, theirs, qt, acc, stat):
     s = shapes_of(grads, theirs)
     outs = (s["queries"], s["flat"], s["row"], s["keys"], s["acc"])
-    scratch = (s["scores"], s["weights"], s["acc"], s["flat"], s["row"])
+    scratch = (s["scores"], s["weights"], s["acc"], s["flat"], s["row"], s["ds"])
     return call(
         second_kernel, "second", outs, scratch, 6 << 30, order, grads, theirs, qt, acc, stat
     )
@@ -336,7 +362,7 @@
         third_kernel,
         "third",
         outs,
-        (s["acc"],),
+        (s["acc"], s["ds"]),
         4 << 30,
         order,
         mine,

time: 123 us -> 121 us (0.984)
  Pallas kernels: 21.1 us -> 18.5 us
  blocking collectives: 89.8 us -> 91.1 us
    pallas_call x3, Pallas kernels: 21.1 us -> 18.5 us  [call(): pl.pallas_call(kernel, out_shape=tuple((jax.ShapeDtypeStruct(*out) for ou...]
    all_to_all x1, blocking collectives: 38.2 us -> 39.6 us  [per_device(): got = lax.all_to_all(total, SPREAD, split_axis=0, concat_axis=0, tiled=True)]
  transfers between devices with their start and end apart: 2 -> 2, of which waited for: 0 -> 0; matrix products, arithmetic and copies ran while one was open for 0% -> 0% of each run, Pallas kernels for 9% -> 8%
where the time goes in v8:
time: 121 us; the launch traced here: 120 us
  blocking collectives  91.1 us (75%)
  Pallas kernels  18.5 us (15%)
  starting transfers between devices  7.01 us (6%)
  other arithmetic  1.22 us (1%)
    all_to_all x1, blocking collectives, per_device(): mine = lax.all_to_all(sent, SPREAD, split_axis=0, concat_axis=0, tiled=True)  51.5 us
    all_to_all x1, blocking collectives, per_device(): got = lax.all_to_all(total, SPREAD, split_axis=0, concat_axis=0, tiled=True)  39.6 us
    pallas_call x3, Pallas kernels, call(): pl.pallas_call(kernel, out_shape=tuple((jax.ShapeDtypeStruct(*out) for ou...  18.5 us
    ppermute x1, starting transfers between devices, per_device(): theirs = lax.ppermute(mine, 'core', SWAP)  5.1 us
  transfers between devices with their start and end apart: 2, of which 0 were waited for; matrix products, arithmetic and copies ran while one was open for 0% of the time, Pallas kernels for 8%

profile of v8, /device:TPU:1, one launch (start us, length us, event | category | flops | bytes accessed | tf_op | source)
XLA Modules:
  0.0 119.5 jit_solution(12607472459175533793)
XLA Ops:
  0.6 0.0 copy-start.2
  0.6 0.0 copy-start
  0.7 0.8 pad_maximum_fusion
  1.4 0.2 broadcast_in_dim.8
  1.7 51.5 %all_to_all.10 = bf16[256,2,8,128]{3,2,1,0:T(8,128)(2,1)S(1)} all-to-all(bf16[256,2,8,128]{3,2,1,0:T(8,128)(2,1)S(1)} %bitcast.19), channel_id=1, replica_groups=mesh['zl'=4,'xh'=2,'xl'=2,'core'=2,'y'=8,'zh'=2] {'y','zl','xh','xl','zh'}, dimensions={0} | all-to-all | bytes 2097152 | tf_op jit(solution)/shard_map/all_to_all | solution.py:394
  53.2 0.0 copy-start.1
  53.2 5.1 %collective-permute-start = (bf16[8,16,2,2,8,128]{5,4,3,2,1,0:T(8,128)(2,1)S(1)}, bf16[8,16,2,2,8,128]{5,4,3,2,1,0:T(8,128)(2,1)S(1)}, u32[]{:S(2)}, u32[]{:S(2)}) collective-permute-start(bf16[8,16,2,2,8,128]{5,4,3,2,1,0:T(8,128)(2,1)S(1)} %bitcast.15), channel_id=1, source_target_pairs={{0,16},{16,0},{1,17},{17,1},{2,18},{18,2},{3,19},{19,3},{4,20},{20... | collective-permute-start | bytes 3145736 | tf_op jit(solution)/shard_map/ppermute | solution.py:396
  58.3 0.0 copy-done.2
  58.3 0.0 copy-done
  58.3 4.1 %first.1 = (bf16[8,128,128]{2,1,0:T(8,128)(2,1)S(1)}, bf16[12,4,256,128]{3,2,1,0:T(8,128)(2,1)S(1)}, f32[2,128,512]{2,1,0:T(8,128)S(1)}, f32[4,1,512]{2,1,0:T(1,128)S(1)}) custom-call(s32[32]{0:T(128)S(1)} %copy-done.2, bf16[256,512]{1,0:T(8,128)(2,1)S(1)} %copy-done, bf16[8,16,2,2,8,128]{5,4,3,2,1,0:T(8,128)(2,1)S(1)} %bitcast.16), custom_call_target="tpu_custom_call" | custom-call | flops 3221225472 | bytes 8388608 | tf_op jit(solution)/shard_map/first/pallas_call | solution.py:308
  62.5 0.0 collective-permute-done.keys_ref
  62.5 0.0 copy-done.1
  62.5 9.3 %second.1 = (bf16[256,512]{1,0:T(8,128)(2,1)}, bf16[8,128,128]{2,1,0:T(8,128)(2,1)S(1)}, f32[2,1,512]{2,1,0:T(1,128)S(1)}, bf16[8,16,2,2,8,128]{5,4,3,2,1,0:T(8,128)(2,1)S(1)}, f32[2,128,512]{2,1,0:T(8,128)S(1)}) custom-call(s32[32]{0:T(128)S(1)} %copy-done.2, bf16[256,512]{1,0:T(8,128)(2,1)S(1)} %copy-done.1, ...), custom_call_target="tpu_custom_call" | custom-call | flops 6442450944 | bytes 8388608 | tf_op jit(solution)/shard_map/second/pallas_call | solution.py:308
  71.8 1.9 %collective-permute-start.1 = (bf16[8,16,2,2,8,128]{5,4,3,2,1,0:T(8,128)(2,1)S(1)}, bf16[8,16,2,2,8,128]{5,4,3,2,1,0:T(8,128)(2,1)S(1)}, u32[]{:S(2)}, u32[]{:S(2)}) collective-permute-start(bf16[8,16,2,2,8,128]{5,4,3,2,1,0:T(8,128)(2,1)S(1)} %get-tuple-element.25), channel_id=1, source_target_pairs={{0,16},{16,0},{1,17},{17,1},{2,18},{18,2},{3,19},{19,3},{4,20},{20... | collective-permute-start | bytes 3145736 | tf_op jit(solution)/shard_map/ppermute | solution.py:402
  73.7 5.1 %third.1 = (bf16[8,16,2,2,8,128]{5,4,3,2,1,0:T(8,128)(2,1)S(1)}, bf16[256,512]{1,0:T(8,128)(2,1)}) custom-call(s32[32]{0:T(128)S(1)} %copy-done.2, bf16[8,16,2,2,8,128]{5,4,3,2,1,0:T(8,128)(2,1)S(1)} %bitcast.17, bf16[8,128,128]{2,1,0:T(8,128)(2,1)S(1)} %get-tuple-element.15.qt_ref, bf16[8,128,128]{2,1,0:T(8,128)(2,1)S(1)} %get-tuple-element.19.gt_ref, ...), custom_call_target="tpu_custom_call" | custom-call | flops 4294967296 | bytes 8388608 | tf_op jit(solution)/shard_map/third/pallas_call | solution.py:308
  78.8 0.0 collective-permute-done.1
  78.8 0.3 add_convert_fusion
  79.1 39.6 %all_to_all.11 = bf16[256,2,8,128]{3,2,1,0:T(8,128)(2,1)S(1)} all-to-all(bf16[256,2,8,128]{3,2,1,0:T(8,128)(2,1)S(1)} %bitcast.18), channel_id=1, replica_groups=mesh['zl'=4,'xh'=2,'xl'=2,'core'=2,'y'=8,'zh'=2] {'y','zl','xh','xl','zh'}, dimensions={0} | all-to-all | bytes 2097152 | tf_op jit(solution)/shard_map/all_to_all | solution.py:408
  118.7 0.2 convert_reduce_fusion
  118.9 0.6 slice_bitcast_fusion
  (1 shorter events, 0.0 us)
Async XLA Ops:
  0.6 57.7 %copy-start.2 = (s32[32]{0:T(128)S(1)}, s32[32]{0:T(128)}, u32[]{:S(2)}) copy-start(s32[32]{0:T(128)} %order_ref.5) | copy-start | bytes 388
  0.6 57.7 %copy-start = (bf16[256,512]{1,0:T(8,128)(2,1)S(1)}, bf16[256,512]{1,0:T(8,128)(2,1)}, u32[]{:S(2)}) copy-start(bf16[256,512]{1,0:T(8,128)(2,1)} %q_ref.1) | copy-start | bytes 786436
  53.2 9.3 %copy-start.1 = (bf16[256,512]{1,0:T(8,128)(2,1)S(1)}, bf16[256,512]{1,0:T(8,128)(2,1)}, u32[]{:S(2)}) copy-start(bf16[256,512]{1,0:T(8,128)(2,1)} %g_ref.1) | copy-start | bytes 786436
  53.2 9.3 %collective-permute-start = (bf16[8,16,2,2,8,128]{5,4,3,2,1,0:T(8,128)(2,1)S(1)}, bf16[8,16,2,2,8,128]{5,4,3,2,1,0:T(8,128)(2,1)S(1)}, u32[]{:S(2)}, u32[]{:S(2)}) collective-permute-start(bf16[8,16,2,2,8,128]{5,4,3,2,1,0:T(8,128)(2,1)S(1)} %bitcast.15), channel_id=1, source_target_pairs={{0,16},{16,0},{1,17},{17,1},{2,18},{18,2},{3,19},{19,3},{4,20},{20... | collective-permute-start | bytes 3145736 | tf_op jit(solution)/shard_map/ppermute | solution.py:396
  71.8 7.0 %collective-permute-start.1 = (bf16[8,16,2,2,8,128]{5,4,3,2,1,0:T(8,128)(2,1)S(1)}, bf16[8,16,2,2,8,128]{5,4,3,2,1,0:T(8,128)(2,1)S(1)}, u32[]{:S(2)}, u32[]{:S(2)}) collective-permute-start(bf16[8,16,2,2,8,128]{5,4,3,2,1,0:T(8,128)(2,1)S(1)} %get-tuple-element.25), channel_id=1, source_target_pairs={{0,16},{16,0},{1,17},{17,1},{2,18},{18,2},{3,19},{19,3},{4,20},{20... | collective-permute-start | bytes 3145736 | tf_op jit(solution)/shard_map/ppermute | solution.py:402
